TPU v7x, 1024 devices: a whole 4x8x16 slice. The times are simulated.
1024 devices in a mesh: panel: 2 (over core), rad: 32 (over y_lo, z), ang: 16 (over y_hi, x).
Axes of the slice: x: 4, y: 8 (y_hi: 4, y_lo: 2; y = y_hi * 2 + y_lo), z: 16, core: 2. Of those that a mesh axis runs over, the one named last changes fastest.
Arguments:
- state: float32 [2, 6, 128, 64, 384], P('panel', None, 'rad', 'ang'), may hold values from 0.25 to 4
- velocity: float32 [2, 3, 128, 64, 384], P('panel', None, 'rad', 'ang'), may hold values from -1 to 1
- band_donor: int32 [2, 1792], replicated, may hold values from 770 to 23420, as said below
- band_weight: float32 [2, 4, 1792], replicated, may hold values from 0 to 1, as said below
Outputs:
- updated: float32 [2, 6, 128, 64, 384], P('panel', None, 'rad', 'ang')
Inputs may be any that keep to these rules, and one draw needn't show every extreme that they name: band_donor[p, t] = row * 384 + col names the donor cells (row, col), (row, col + 1), (row + 1, col), (row + 1, col + 1) in the panel other than p, with row from 2 to 60 and col from 2 to 380. `band_weight`: the four weights of a zone are products of two factors in [0, 1], in the order of the donor cells, and sum to 1.
All inputs are finite; a program needn't handle non-finite values.
Results may differ from a plain program's by a relative error of at most 0.0003.
Values sent between devices are 32-bit elements; how exact they have to be, the bound alone decides.
A program may use at most 64 MiB of HBM per device.

v0:
```python
import math

import jax
import jax.numpy as jnp
from jax import lax
from jax.sharding import PartitionSpec as P

G = 2


inner_radius = 1.0
courant_limit = 0.8


def padded_2(value, sides, width):
    for axis, dim in sides:
        size, length = (lax.axis_size(axis), value.shape[dim])
        up = [(i, (i + 1) % size) for i in range(size - 1)]
        down = [(j, i) for i, j in up]
        last = lax.slice_in_dim(value, length - width, length, axis=dim)
        first = lax.slice_in_dim(value, 0, width, axis=dim)
        before = lax.ppermute(last, axis, up)
        after = lax.ppermute(first, axis, down)
        value = jnp.concatenate([before, value, after], axis=dim)
    return value


def geometry(theta_cells, phi_cells):
    theta_step = math.pi / 2 / (theta_cells - 2 * G)
    phi_step = 1.5 * math.pi / (phi_cells - 2 * G)
    radius_step = inner_radius * theta_step
    theta_start = math.pi / 4 - G * theta_step
    time_step = courant_limit * inner_radius * min(theta_step, math.sin(theta_start) * phi_step)
    return (theta_step, phi_step, radius_step, theta_start, time_step)


def window(values, first_cell, how_many, direction):
    return lax.slice_in_dim(values, first_cell, first_cell + how_many, axis=direction)


def transport(values, motion, direction, face_area, face_rate, cell_rate):
    cells = values.shape[direction] - 6
    left_cells = window(values, 1, cells + 3, direction)
    right_cells = window(values, 2, cells + 3, direction)
    interface = 7.0 / 12.0 * (left_cells + right_cells) - 1.0 / 12.0 * (
        window(values, 0, cells + 3, direction) + window(values, 3, cells + 3, direction)
    )
    interface = jnp.clip(
        interface, jnp.minimum(left_cells, right_cells), jnp.maximum(left_cells, right_cells)
    )
    left_edge = window(interface, 0, cells + 2, direction)
    right_edge = window(interface, 1, cells + 2, direction)
    middle = window(values, 2, cells + 2, direction)
    spread = right_edge - left_edge
    curvature = 6.0 * (middle - 0.5 * (left_edge + right_edge))
    face_speed = 0.5 * (
        window(motion, 2, cells + 1, direction) + window(motion, 3, cells + 1, direction)
    )
    courant = jnp.abs(face_speed) * face_rate
    keeping = 1.0 - 2.0 / 3.0 * courant
    from_left = window(right_edge, 0, cells + 1, direction) - 0.5 * courant * (
        window(spread, 0, cells + 1, direction)
        - keeping * window(curvature, 0, cells + 1, direction)
    )
    from_right = window(left_edge, 1, cells + 1, direction) + 0.5 * courant * (
        window(spread, 1, cells + 1, direction)
        + keeping * window(curvature, 1, cells + 1, direction)
    )
    face_flux = face_area * face_speed * jnp.where(face_speed > 0, from_left, from_right)
    return window(values, 3, cells, direction) - cell_rate * (
        window(face_flux, 1, cells, direction) - window(face_flux, 0, cells, direction)
    )


def edge_pad(values, direction):
    widths = [(0, 0)] * values.ndim
    widths[direction] = (3, 3)
    return jnp.pad(values, widths, mode="edge")


def fix_ghosts(extended, initial, direction, first_device, last_device):
    lower_ghost = jnp.where(
        first_device,
        jnp.repeat(window(initial, 0, 1, direction), 3, axis=direction),
        window(extended, 0, 3, direction),
    )
    cells = initial.shape[direction]
    upper_ghost = jnp.where(
        last_device,
        jnp.repeat(window(initial, cells - 1, 1, direction), 3, axis=direction),
        window(extended, cells + 3, 3, direction),
    )
    return jnp.concatenate([lower_ghost, initial, upper_ghost], axis=direction)


def body(state, velocity, band_donor, band_weight):
    values = state[0]
    motion = velocity[0]
    fields_count, rows_dev, theta_dev, phi_cells = values.shape
    rad_devices = lax.axis_size("rad")
    ang_devices = lax.axis_size("ang")
    radial_cells = rows_dev * rad_devices
    theta_cells = theta_dev * ang_devices
    shell_index = lax.axis_index("rad")
    tile_index = lax.axis_index("ang")
    panel_index = lax.axis_index("panel")
    theta_step, phi_step, radius_step, theta_start, time_step = geometry(theta_cells, phi_cells)
    radial_step = time_step / radius_step
    radius_cell = (
        inner_radius
        + ((shell_index * rows_dev + jnp.arange(rows_dev)).astype(jnp.float32) + 0.5) * radius_step
    )
    stacked = jnp.concatenate([values, motion[0:1]], axis=0)
    flat_block = stacked.reshape(fields_count + 1, rows_dev, theta_dev * phi_cells)
    pencil = lax.all_to_all(flat_block, "rad", split_axis=2, concat_axis=1, tiled=True)
    padded = edge_pad(pencil, 1)
    radius_face = inner_radius + jnp.arange(radial_cells + 1).astype(jnp.float32) * radius_step
    column_radius = (
        inner_radius + (jnp.arange(radial_cells).astype(jnp.float32) + 0.5) * radius_step
    )
    radial_area = (radius_face * radius_face)[:, None]
    radial_rate = (time_step / (column_radius * column_radius * radius_step))[:, None]
    radial_done = transport(
        padded[:fields_count], padded[fields_count:], 1, radial_area, radial_step, radial_rate
    )
    returned = lax.all_to_all(radial_done, "rad", split_axis=1, concat_axis=2, tiled=True)
    after_radial = returned.reshape(fields_count, rows_dev, theta_dev, phi_cells)
    theta_face = (
        theta_start
        + (tile_index * theta_dev + jnp.arange(theta_dev + 1)).astype(jnp.float32) * theta_step
    )
    theta_cell = (
        theta_start
        + ((tile_index * theta_dev + jnp.arange(theta_dev)).astype(jnp.float32) + 0.5) * theta_step
    )
    polar_area = jnp.sin(theta_face)[:, None]
    polar_step = (time_step / (radius_cell * theta_step))[:, None, None]
    polar_rate = (time_step / (radius_cell[:, None] * jnp.sin(theta_cell)[None, :] * theta_step))[
        :, :, None
    ]
    azimuth_rate = (time_step / (radius_cell[:, None] * jnp.sin(theta_cell)[None, :] * phi_step))[
        :, :, None
    ]
    polar_stack = jnp.concatenate([after_radial, motion[1:2]], axis=0)
    polar_extended = padded_2(polar_stack, (("ang", 2),), 3)
    polar_extended = fix_ghosts(
        polar_extended, polar_stack, 2, tile_index == 0, tile_index == ang_devices - 1
    )
    after_polar = transport(
        polar_extended[:fields_count],
        polar_extended[fields_count:],
        2,
        polar_area,
        polar_step,
        polar_rate,
    )
    after_azimuth = transport(
        edge_pad(after_polar, 3), edge_pad(motion[2:3], 3), 3, 1.0, azimuth_rate, azimuth_rate
    )
    cells_tile = theta_dev * phi_cells
    flat_swept = after_azimuth.reshape(fields_count, rows_dev, cells_tile)
    twin_panel = 1 - panel_index
    donor_cell = lax.dynamic_index_in_dim(band_donor, twin_panel, 0, keepdims=False)
    weights = lax.dynamic_index_in_dim(band_weight, twin_panel, 0, keepdims=False)
    tile_start = tile_index * cells_tile
    contribution = jnp.zeros((fields_count, rows_dev, donor_cell.shape[0]), jnp.float32)
    for corner, offset in enumerate((0, 1, phi_cells, phi_cells + 1)):
        local_index = donor_cell + offset - tile_start
        inside = (local_index >= 0) & (local_index < cells_tile)
        picked = jnp.take(flat_swept, jnp.clip(local_index, 0, cells_tile - 1), axis=2)
        contribution = contribution + jnp.where(inside, weights[corner], 0.0) * picked
    theta_zones = 2 * G * phi_cells
    phi_per_tile = 2 * G * theta_dev
    panel_slots = jnp.stack(
        [
            jnp.where(panel_index == 1, contribution, 0.0),
            jnp.where(panel_index == 0, contribution, 0.0),
        ]
    )
    summed = lax.psum(panel_slots, ("panel", "ang"))
    own_values = lax.dynamic_index_in_dim(summed, panel_index, 0, keepdims=False)
    theta_values = own_values[:, :, :theta_zones]
    phi_values = lax.dynamic_slice_in_dim(
        own_values, theta_zones + tile_index * phi_per_tile, phi_per_tile, axis=2
    )
    phi_block = phi_values.reshape(fields_count, rows_dev, theta_dev, 2 * G)
    result = jnp.concatenate(
        [phi_block[..., :G], after_azimuth[..., G : phi_cells - G], phi_block[..., G:]], axis=3
    )
    top_rows = theta_values[:, :, : G * phi_cells].reshape(fields_count, rows_dev, G, phi_cells)
    bottom_rows = theta_values[:, :, G * phi_cells :].reshape(fields_count, rows_dev, G, phi_cells)
    upper_rows = jnp.where(tile_index == 0, top_rows, result[:, :, :G])
    lower_rows = jnp.where(
        tile_index == ang_devices - 1, bottom_rows, result[:, :, theta_dev - G :]
    )
    result = jnp.concatenate([upper_rows, result[:, :, G : theta_dev - G], lower_rows], axis=2)
    return result[None]


def solution(mesh):
    in_specs = (
        P("panel", None, "rad", "ang", None),
        P("panel", None, "rad", "ang", None),
        P(),
        P(),
    )
    out_specs = P("panel", None, "rad", "ang", None)
    return jax.shard_map(body, mesh=mesh, in_specs=in_specs, out_specs=out_specs, check_vma=False)
```

profile of v0, /device:TPU:40, one launch (start us, length us, event | category | flops | bytes accessed | tf_op | source)
XLA Modules:
  0.0 477.2 jit_solution(9062230684003154331)
XLA Ops:
  6.5 0.8 slice_bitcast_fusion
  7.3 1.0 concatenate.58
  8.4 1.3 copy.40
  9.7 4.3 reshape.400
  14.0 20.4 %all-to-all-start = ((f32[32,1,1344]{2,1,0:T(1,128)}), f32[32,1,1344]{2,1,0:T(1,128)S(1)}, u32[]{:S(2)}, u32[]{:S(2)}) async-start(f32[32,1,1344]{2,1,0:T(1,128)} %reshape.400), calls=%async_computation | async-start | bytes 360448 | tf_op jit(solution)/shard_map/all_to_all | solution.py:115
  34.5 0.1 clamp_reduce_fusion.3
  34.7 0.1 slice_reduce_fusion.1
  35.0 17.1 %all-to-all-done = f32[32,1,1344]{2,1,0:T(1,128)S(1)} async-done(((f32[32,1,1344]{2,1,0:T(1,128)}), f32[32,1,1344]{2,1,0:T(1,128)S(1)}, u32[]{:S(2)}, u32[]{:S(2)}) %all-to-all-start) | async-done | bytes 172064 | tf_op jit(solution)/shard_map/all_to_all | solution.py:115
  52.0 0.6 broadcast.493
  52.6 1.1 reduce.20
  53.7 4.0 reshape.401
  57.8 2.5 copy.54
  60.3 1.3 copy.43
  61.8 1.0 slice.389
  62.8 0.2 fusion.16
  63.0 0.1 slice_subtract_fusion.2
  63.2 0.3 copy.42
  63.4 0.1 multiply_bitcast_fusion.1
  63.5 0.2 fusion.7
  63.8 0.1 fusion.18
  63.9 0.2 copy.68
  64.1 1.0 reshape.402
  65.2 5.1 %all-to-all-start.1 = ((f32[32,1,1152]{2,1,0:T(1,128)}), f32[32,1,1152]{2,1,0:T(1,128)S(1)}, u32[]{:S(2)}, u32[]{:S(2)}) async-start(f32[32,1,1152]{2,1,0:T(1,128)} %reshape.402), calls=%async_computation.1 | async-start | bytes 294912 | tf_op jit(solution)/shard_map/all_to_all | solution.py:126
  70.5 0.1 compare_bitcast_fusion.2
  70.6 0.1 multiply_bitcast_fusion.4
  70.7 14.5 %all-to-all-done.1 = f32[32,1,1152]{2,1,0:T(1,128)S(1)} async-done(((f32[32,1,1152]{2,1,0:T(1,128)}), f32[32,1,1152]{2,1,0:T(1,128)S(1)}, u32[]{:S(2)}, u32[]{:S(2)}) %all-to-all-start.1) | async-done | bytes 147488 | tf_op jit(solution)/shard_map/all_to_all | solution.py:126
  85.3 1.0 reduce.21
  86.3 0.3 reshape.403
  86.7 0.2 reshape.333
  87.0 3.4 collective-permute-start
  90.5 0.1 fusion.55
  90.7 6.8 %collective-permute-start.1 = (f32[7,4,3,384]{3,2,1,0:T(4,128)S(1)}, f32[7,4,3,384]{3,2,1,0:T(4,128)S(1)}, u32[]{:S(2)}, u32[]{:S(2)}) collective-permute-start(f32[7,4,3,384]{3,2,1,0:T(4,128)S(1)} %get-tuple-element.35), channel_id=1, source_target_pairs={{1,0},{2,1},{3,2},{4,3},{5,4},{6,5},{7,6},{8,7},{9,8},{10,9},{11,1... | collective-permute-start | bytes 387080 | tf_op jit(solution)/shard_map/ppermute | solution.py:23
  97.6 2.8 collective-permute-done
  100.4 1.6 collective-permute-done.1
  102.1 0.2 pad_maximum_fusion
  102.3 0.2 fusion.32
  102.5 0.1 slice_subtract_fusion.4
  102.7 0.2 fusion.23
  102.9 0.1 fusion.50
  103.1 0.3 copy.55
  103.3 0.3 copy.56
  103.8 0.2 pad_maximum_fusion.9
  104.0 0.4 fusion.45
  104.4 0.3 slice_subtract_fusion.6
  104.6 0.4 fusion.37
  105.0 0.2 fusion.48
  105.2 1.4 copy.51
  106.6 6.3 %gather_fusion = f32[1792,6,4]{1,2,0:T(4,128)} fusion(f32[6,4,1536]{0,1,2:T(4,128)S(1)} %bitcast.112, s32[2048]{0:T(1024)S(1)} %pad_clamp_fusion.3), kind=kCustom, calls=%fused_computation.clone | custom fusion | bytes 351232 | tf_op jit(solution)/shard_map/jit(_take)/gather | solution.py:170
  112.9 6.4 %gather_fusion.1 = f32[1792,6,4]{1,2,0:T(4,128)} fusion(f32[6,4,1536]{0,1,2:T(4,128)S(1)} %bitcast.113, s32[2048]{0:T(1024)S(1)} %pad_clamp_fusion.2), kind=kCustom, calls=%fused_computation.1.clone | custom fusion | bytes 351232 | tf_op jit(solution)/shard_map/jit(_take)/gather | solution.py:170
  119.3 6.3 %gather_fusion.2 = f32[1792,6,4]{1,2,0:T(4,128)} fusion(f32[6,4,1536]{0,1,2:T(4,128)S(1)} %bitcast.114, s32[2048]{0:T(1024)S(1)} %pad_clamp_fusion.1), kind=kCustom, calls=%fused_computation.2.clone | custom fusion | bytes 351232 | tf_op jit(solution)/shard_map/jit(_take)/gather | solution.py:170
  125.5 6.4 %gather_fusion.3 = f32[1792,6,4]{1,2,0:T(4,128)} fusion(f32[6,4,1536]{0,1,2:T(4,128)S(1)} %bitcast.115, s32[2048]{0:T(1024)S(1)} %pad_clamp_fusion), kind=kCustom, calls=%fused_computation.3.clone | custom fusion | bytes 351232 | tf_op jit(solution)/shard_map/jit(_take)/gather | solution.py:170
  131.9 20.2 %select_bitcast_fusion.1 = (f32[1,6,4,1792]{1,2,3,0:T(4,128)}, f32[6,4,1792]{0,1,2:T(4,128)S(1)}) fusion(pred[]{:T(512)S(6)} %eq.15, f32[1792,6,4]{1,2,0:T(4,128)} %gather_fusion.3, pred[1792]{0:T(1024)(128)(4,1)S(1)} %get-tuple-element.64, f32[1792]{0:T(1024)S(1)} %get-tuple-element.9, f32[1792,6,4]{1,2,0:T(4,128)} %gather_fusion.2, ...), kind=kLoop, calls=%fused_computation.12 | loop fusion | flops 516096 | bytes 1068033 | tf_op jit(solution)/shard_map/stack | solution.py:174
  152.1 2.2 select_bitcast_fusion
  154.4 3.4 copy.53
  157.7 3.4 copy.52
  161.1 0.8 pad_maximum_fusion.4
  162.0 0.1 slice.440
  162.1 305.2 %all-reduce.2.cloned.1.call-done = f32[2,6,4,1792]{3,2,1,0:T(4,128)} async-done(((f32[2,6,4,1792]{3,2,1,0:T(4,128)}), f32[2,6,4,1792]{3,2,1,0:T(4,128)}) %all-reduce.2.cloned.1.call-update) | async-done | bytes 344080 | tf_op jit(solution)/shard_map/psum | solution.py:180
  467.3 0.8 constant_dynamic-slice_fusion
  468.1 0.1 reshape.342
  468.3 0.9 dynamic-slice_bitcast_fusion
  469.3 0.2 pad_maximum_fusion.12
  469.5 0.1 slice_select_fusion.1
  469.6 0.7 maximum_bitcast_fusion
  (47 shorter events, 1.6 us)
Async XLA Ops:
  8.3 26.1 %copy-start = (s32[2,1792]{1,0:T(2,128)S(1)}, s32[2,1792]{1,0:T(2,128)}, u32[]{:S(2)}) copy-start(s32[2,1792]{1,0:T(2,128)} %param.8) | copy-start | bytes 43012
  14.0 38.0 %all-to-all-start = ((f32[32,1,1344]{2,1,0:T(1,128)}), f32[32,1,1344]{2,1,0:T(1,128)S(1)}, u32[]{:S(2)}, u32[]{:S(2)}) async-start(f32[32,1,1344]{2,1,0:T(1,128)} %reshape.400), calls=%async_computation | async-start | bytes 360448 | tf_op jit(solution)/shard_map/all_to_all | solution.py:115
  63.8 26.7 %copy-start.1 = (f32[2,4,1792]{2,1,0:T(4,128)S(1)}, f32[2,4,1792]{2,1,0:T(4,128)}, u32[]{:S(2)}) copy-start(f32[2,4,1792]{2,1,0:T(4,128)} %param.9) | copy-start | bytes 172036
  65.2 20.1 %all-to-all-start.1 = ((f32[32,1,1152]{2,1,0:T(1,128)}), f32[32,1,1152]{2,1,0:T(1,128)S(1)}, u32[]{:S(2)}, u32[]{:S(2)}) async-start(f32[32,1,1152]{2,1,0:T(1,128)} %reshape.402), calls=%async_computation.1 | async-start | bytes 294912 | tf_op jit(solution)/shard_map/all_to_all | solution.py:126
  70.3 397.0 %all-reduce.2.cloned.1.call-start = ((), (), s32[]{:S(2)}) async-start(), calls=%async_computation.2 | async-start | bytes 688128 | tf_op jit(solution)/shard_map/psum | solution.py:180
  87.0 13.4 %collective-permute-start = (f32[7,4,3,384]{3,2,1,0:T(4,128)S(1)}, f32[7,4,3,384]{3,2,1,0:T(4,128)S(1)}, u32[]{:S(2)}, u32[]{:S(2)}) collective-permute-start(f32[7,4,3,384]{3,2,1,0:T(4,128)S(1)} %get-tuple-element.34), channel_id=1, source_target_pairs={{0,1},{1,2},{2,3},{3,4},{4,5},{5,6},{6,7},{7,8},{8,9},{9,10},{10,1... | collective-permute-start | bytes 387080 | tf_op jit(solution)/shard_map/ppermute | solution.py:22
  90.7 11.3 %collective-permute-start.1 = (f32[7,4,3,384]{3,2,1,0:T(4,128)S(1)}, f32[7,4,3,384]{3,2,1,0:T(4,128)S(1)}, u32[]{:S(2)}, u32[]{:S(2)}) collective-permute-start(f32[7,4,3,384]{3,2,1,0:T(4,128)S(1)} %get-tuple-element.35), channel_id=1, source_target_pairs={{1,0},{2,1},{3,2},{4,3},{5,4},{6,5},{7,6},{8,7},{9,8},{10,9},{11,1... | collective-permute-start | bytes 387080 | tf_op jit(solution)/shard_map/ppermute | solution.py:23
Sparse Core Ops, SparseCore 0:
  162.1 305.1 all-reduce.1
where the time goes:
time: 478 us; the launch traced here: 477 us
  waiting for transfers between devices  341 us (71%)
  local copies, waits for them, and re-layouts  55.7 us (12%)
  starting transfers between devices  35.8 us (7%)
  other arithmetic  30.6 us (6%)
  between operations  14 us (3%)
    psum x1, waiting for transfers between devices, body(): summed = lax.psum(panel_slots, ('panel', 'ang'))  305 us
    gather x4, local copies, waits for them, and re-layouts, body(): jnp.take(flat_swept, jnp.clip(local_index, 0, cells_tile - 1), axis=2)  25.3 us
    another operation x3, other arithmetic, body(): jnp.stack([jnp.where(panel_index == 1, contribution, 0.0), jnp.where(pane...  23.3 us
    all_to_all x1, starting transfers between devices, body(): lax.all_to_all(flat_block, 'rad', split_axis=2, concat_axis=1, tiled=True)  20.4 us
    all_to_all x1, waiting for transfers between devices, body(): lax.all_to_all(flat_block, 'rad', split_axis=2, concat_axis=1, tiled=True)  17.1 us
    all_to_all x1, waiting for transfers between devices, body(): lax.all_to_all(radial_done, 'rad', split_axis=1, concat_axis=2, tiled=True)  14.5 us
    unnamed x11, local copies, waits for them, and re-layouts  9.71 us
  transfers between devices with their start and end apart: 5, of which 5 were waited for; matrix products, arithmetic and copies ran while one was open for 0% of the time, Pallas kernels for 0%

commit v1 on v0

v1 whole, which is shorter than its diff:
```python
import functools
import math

import jax
import jax.numpy as jnp
from jax import lax
from jax.experimental import pallas as pl
from jax.experimental.pallas import tpu as pltpu
from jax.sharding import PartitionSpec as P

G = 2
INNER_RADIUS = 1.0
COURANT = 0.8
MESH = pl.DeviceIdType.MESH
F32 = jnp.float32
BF16 = jnp.bfloat16


def geometry(theta_cells, phi_cells):
    theta_step = math.pi / 2 / (theta_cells - 2 * G)
    phi_step = 1.5 * math.pi / (phi_cells - 2 * G)
    radius_step = INNER_RADIUS * theta_step
    theta_start = math.pi / 4 - G * theta_step
    time_step = COURANT * INNER_RADIUS * min(theta_step, math.sin(theta_start) * phi_step)
    return theta_step, phi_step, radius_step, theta_start, time_step


def flux_coefficients(face_speed, area, face_rate):
    size = jnp.abs(face_speed)
    courant = size * face_rate
    half = 0.5 * courant
    a0 = face_speed if area is None else area * face_speed
    a1 = a0 * (half * (1.0 - 2.0 / 3.0 * courant))
    a2 = -(half * (size if area is None else area * size))
    return a0, a1, a2


def clipped_interface(before, left, right, after):
    value = 7.0 / 12.0 * (left + right) - 1.0 / 12.0 * (before + after)
    return jnp.minimum(jnp.maximum(value, jnp.minimum(left, right)), jnp.maximum(left, right))


def sweep_leading(q, a0, a1, a2, rate):
    n = q.shape[0] - 6
    face = clipped_interface(q[0 : n + 3], q[1 : n + 4], q[2 : n + 5], q[3 : n + 6])
    left, right = face[0 : n + 2], face[1 : n + 3]
    spread = right - left
    curvature = 6.0 * (q[2 : n + 4] - 0.5 * (left + right))
    up = a0 > 0
    flux = (
        a0 * face[1 : n + 2]
        + a1 * jnp.where(up, curvature[0 : n + 1], curvature[1 : n + 2])
        + a2 * jnp.where(up, spread[0 : n + 1], spread[1 : n + 2])
    )
    return q[3 : n + 3] - rate * (flux[1 : n + 1] - flux[0:n])


def with_ghost_lanes(x):
    rows, cells = x.shape
    lane = lax.broadcasted_iota(jnp.int32, (rows, 128), 1)
    last = jnp.broadcast_to(x[:, cells - 1 : cells], (rows, 128))
    first = jnp.broadcast_to(x[:, 0:1], (rows, 128))
    return jnp.concatenate([x, jnp.where(lane < 64, last, first)], axis=1)


def sweep_lanes(q, a0, a1, a2, rate):
    width = q.shape[1]
    cells = width - 128
    before = pltpu.roll(q, 1, 1)
    face = clipped_interface(pltpu.roll(q, 2, 1), before, q, pltpu.roll(q, width - 1, 1))
    right = pltpu.roll(face, width - 1, 1)
    spread = right - face
    curvature = 6.0 * (q - 0.5 * (face + right))
    up = a0 > 0
    flux = (
        a0 * face
        + a1 * jnp.where(up, pltpu.roll(curvature, 1, 1), curvature)
        + a2 * jnp.where(up, pltpu.roll(spread, 1, 1), spread)
    )
    change = pltpu.roll(flux, width - 1, 1) - flux
    return q[:, :cells] - rate * change[:, :cells]


def put(ref, index, rows, value):
    for c in range(value.shape[1] // 128):
        ref[index, c, rows, :] = value[:, 128 * c : 128 * c + 128]


def get(ref, index, rows):
    return jnp.concatenate([ref[index, c, rows, :] for c in range(ref.shape[1])], axis=1)


def kernel(
    sizes,
    state_hbm,
    velocity_hbm,
    donor_ref,
    weight_ref,
    out_ref,
    own,
    vel,
    rad_ext,
    rad_vel,
    stage,
    ang_ext,
    ang_vel,
    azi_coef,
    swept,
    planes,
    split,
    onehot,
    near_weight,
    far_weight,
    zone_sum,
    theta_out,
    phi_out,
    theta_in,
    phi_in,
    phi_rows,
    local_sem,
    halo_send,
    halo_recv,
    plane_send,
    plane_recv,
    zone_send,
    theta_recv,
    phi_recv,
):
    n_rad, n_ang, groups, nr, nt, nphi, theta_cells, zones = sizes
    panel = lax.axis_index("panel")
    rad = lax.axis_index("rad")
    ang = lax.axis_index("ang")
    twin = 1 - panel
    theta_step, phi_step, radius_step, theta_start, time_step = geometry(theta_cells, nphi)
    first_owner = 2
    owners = groups * nr
    is_owner = (ang >= first_owner) & (ang < first_owner + owners)

    load_state = pltpu.make_async_copy(state_hbm, own, local_sem.at[0])
    load_velocity = pltpu.make_async_copy(velocity_hbm, vel, local_sem.at[1])
    load_state.start()
    load_velocity.start()

    rad_down = (panel, lax.rem(rad + n_rad - 1, n_rad), ang)
    rad_up = (panel, lax.rem(rad + 1, n_rad), ang)
    ang_down = (panel, rad, lax.rem(ang + n_ang - 1, n_ang))
    ang_up = (panel, rad, lax.rem(ang + 1, n_ang))

    barrier = pltpu.get_barrier_semaphore()
    pl.semaphore_signal(barrier, inc=1, device_id=rad_down, device_id_type=MESH)
    pl.semaphore_signal(barrier, inc=1, device_id=rad_up, device_id_type=MESH)
    members = 2 * n_ang
    place = panel * n_ang + ang

    def greet(k, carry):
        other = lax.rem(place + k, members)
        pl.semaphore_signal(
            barrier,
            inc=1,
            device_id=(other // n_ang, rad, lax.rem(other, n_ang)),
            device_id_type=MESH,
        )
        return carry

    lax.fori_loop(1, members, greet, 0)

    load_state.wait()
    load_velocity.wait()
    for g in range(groups):
        for f in range(2):
            for r in range(nr):
                rad_ext[g, 3 + r, f * nt : (f + 1) * nt, :] = own[2 * g + f, r]
    for r in range(nr):
        for f in range(2):
            rad_vel[1 + r, f * nt : (f + 1) * nt, :] = vel[0, r]
            row = (2 * r + f) * nt
            put(stage, groups, pl.ds(row, nt), vel[1, r])
            put(stage, groups + 1, pl.ds(row, nt), vel[2, r])
    for t in range(nt):
        ang_vel[1 + t] = get(stage, groups, pl.ds(t, 2 * nr, stride=nt))

    pl.semaphore_wait(barrier, members + 1)

    def send(src, dst, slot, device):
        return pltpu.make_async_remote_copy(
            src_ref=src,
            dst_ref=dst,
            send_sem=halo_send.at[slot],
            recv_sem=halo_recv.at[slot],
            device_id=device,
            device_id_type=MESH,
        )

    rad_copies, ang_copies = [], []
    for g in range(groups):
        rad_copies.append(
            (
                send(rad_ext.at[g, 3:6], rad_ext.at[g, nr + 3 : nr + 6], 4 * g, rad_down),
                send(rad_ext.at[g, nr : nr + 3], rad_ext.at[g, 0:3], 4 * g + 1, rad_up),
            )
        )
        ang_copies.append(
            (
                send(ang_ext.at[g, 3:6], ang_ext.at[g, nt + 3 : nt + 6], 4 * g + 2, ang_down),
                send(ang_ext.at[g, nt : nt + 3], ang_ext.at[g, 0:3], 4 * g + 3, ang_up),
            )
        )
    base = 4 * groups
    rad_vel_copies = (
        send(rad_vel.at[1], rad_vel.at[nr + 1], base, rad_down),
        send(rad_vel.at[nr], rad_vel.at[0], base + 1, rad_up),
    )
    ang_vel_copies = (
        send(ang_vel.at[1], ang_vel.at[nt + 1], base + 2, ang_down),
        send(ang_vel.at[nt], ang_vel.at[0], base + 3, ang_up),
    )
    for copy in rad_vel_copies + rad_copies[0] + ang_vel_copies:
        copy.start()
    for g in range(1, groups):
        for copy in rad_copies[g]:
            copy.start()

    @pl.when(is_owner)
    def _():
        donor_all = donor_ref[...]
        donor = jnp.where(panel == 0, donor_all[1:2], donor_all[0:1]).astype(F32)
        donor_row = jnp.floor((donor + 0.5) * (1.0 / nphi))
        donor_col = donor - donor_row * nphi
        weights = jnp.where(panel == 0, weight_ref[1], weight_ref[0])
        cells = 2 * theta_cells
        row_of = lax.broadcasted_iota(jnp.int32, (cells, 128), 0)
        row_of = ((row_of // (2 * nt)) * nt + lax.rem(row_of, nt)).astype(F32)
        col_of = lax.broadcasted_iota(jnp.int32, (nphi, 128), 0).astype(F32)
        for z in range(0, zones, 128):
            here = donor_row[:, z : z + 128]
            w = weights[:, z : z + 128]
            at_row = row_of == here
            above = row_of == here + 1.0
            near_weight[:, z : z + 128] = jnp.where(
                at_row, w[0:1], jnp.where(above, w[2:3], 0.0)
            )
            far_weight[:, z : z + 128] = jnp.where(
                at_row, w[1:2], jnp.where(above, w[3:4], 0.0)
            )
            hot = jnp.where(col_of == donor_col[:, z : z + 128], 1.0, 0.0).astype(BF16)
            onehot[0:nphi, z : z + 128] = hot
            onehot[nphi : 2 * nphi, z : z + 128] = hot

    def wide(x, tiles):
        return jnp.concatenate([x] * tiles, axis=-1)

    tiles = nphi // 128
    lead = lambda n: lax.broadcasted_iota(jnp.int32, (n, 8, 128), 0)
    sub = lambda n: lax.broadcasted_iota(jnp.int32, (n, 8, 128), 1)
    radius_of_row = (
        INNER_RADIUS + ((rad * nr + sub(nt) // 2).astype(F32) + 0.5) * radius_step
    )
    theta_cell = theta_start + ((ang * nt + lead(nt)).astype(F32) + 0.5) * theta_step
    sin_cell = jnp.sin(theta_cell)
    polar_rate = wide(time_step / (radius_of_row * sin_cell * theta_step), tiles)
    azimuth_rate = time_step / (radius_of_row * sin_cell * phi_step)
    azimuth_rate = azimuth_rate.reshape(nt * 8, 128)
    azi_u = jnp.concatenate(
        [get(stage, groups + 1, pl.ds(t, 2 * nr, stride=nt)) for t in range(nt)], axis=0
    )
    azi_u = with_ghost_lanes(azi_u)
    azi_face = 0.5 * (azi_u + pltpu.roll(azi_u, 1, 1))
    for i, coefficient in enumerate(
        flux_coefficients(azi_face, None, wide(azimuth_rate, tiles + 1))
    ):
        azi_coef[i] = coefficient
    azimuth_rate = wide(azimuth_rate, tiles)

    for copy in rad_vel_copies:
        copy.wait_recv()
    v = rad_vel[...]
    v_first = jnp.where(rad == 0, v[1:2], v[0:1])
    v_last = jnp.where(rad == n_rad - 1, v[nr : nr + 1], v[nr + 1 : nr + 2])
    v = jnp.concatenate([v_first, v[1 : nr + 1], v_last], axis=0)
    radius_face = INNER_RADIUS + (rad * nr + lead(nr + 1)).astype(F32) * radius_step
    radius_cell = INNER_RADIUS + ((rad * nr + lead(nr)).astype(F32) + 0.5) * radius_step
    rad_coef = flux_coefficients(
        0.5 * (v[0 : nr + 1] + v[1 : nr + 2]),
        wide(radius_face * radius_face, tiles),
        time_step / radius_step,
    )
    rad_rate = wide(time_step / (radius_cell * radius_cell * radius_step), tiles)
    for g in range(groups):
        for copy in rad_copies[g]:
            copy.wait_recv()
        q = rad_ext[g]
        inner = q[3 : nr + 3]
        low = jnp.where(rad == 0, jnp.concatenate([inner[0:1]] * 3, axis=0), q[0:3])
        high = jnp.where(
            rad == n_rad - 1, jnp.concatenate([inner[nr - 1 : nr]] * 3, axis=0), q[nr + 3 : nr + 6]
        )
        after = sweep_leading(jnp.concatenate([low, inner, high], axis=0), *rad_coef, rad_rate)
        for r in range(nr):
            put(stage, g, pl.ds(8 * r, 8), after[r])
        for t in range(nt):
            ang_ext[g, 3 + t] = get(stage, g, pl.ds(t, 2 * nr, stride=nt))
        for copy in ang_copies[g]:
            copy.start()

    for copy in ang_vel_copies:
        copy.wait_recv()
    v = ang_vel[...]
    v_first = jnp.where(ang == 0, v[1:2], v[0:1])
    v_last = jnp.where(ang == n_ang - 1, v[nt : nt + 1], v[nt + 1 : nt + 2])
    v = jnp.concatenate([v_first, v[1 : nt + 1], v_last], axis=0)
    theta_face = theta_start + (ang * nt + lead(nt + 1)).astype(F32) * theta_step
    radius_of_face = INNER_RADIUS + ((rad * nr + sub(nt + 1) // 2).astype(F32) + 0.5) * radius_step
    ang_coef = flux_coefficients(
        0.5 * (v[0 : nt + 1] + v[1 : nt + 2]),
        wide(jnp.sin(theta_face), tiles),
        wide(time_step / (radius_of_face * theta_step), tiles),
    )

    def plane_copy(g, r):
        return pltpu.make_async_remote_copy(
            src_ref=swept.at[g, :, 8 * r : 8 * r + 8],
            dst_ref=planes.at[ang],
            send_sem=plane_send.at[g * nr + r],
            recv_sem=plane_recv,
            device_id=(panel, rad, first_owner + g * nr + r),
            device_id_type=MESH,
        )

    for g in range(groups):
        for copy in ang_copies[g]:
            copy.wait_recv()
        q = ang_ext[g]
        inner = q[3 : nt + 3]
        low = jnp.where(ang == 0, jnp.concatenate([inner[0:1]] * 3, axis=0), q[0:3])
        high = jnp.where(
            ang == n_ang - 1, jnp.concatenate([inner[nt - 1 : nt]] * 3, axis=0), q[nt + 3 : nt + 6]
        )
        polar = sweep_leading(jnp.concatenate([low, inner, high], axis=0), *ang_coef, polar_rate)
        cells = with_ghost_lanes(polar.reshape(nt * 8, nphi))
        done = sweep_lanes(cells, azi_coef[0], azi_coef[1], azi_coef[2], azimuth_rate)
        for t in range(nt):
            put(swept, g, pl.ds(t, 2 * nr, stride=nt), done[8 * t : 8 * t + 8])
        for r in range(nr):
            @pl.when(ang != first_owner + g * nr + r)
            def _():
                plane_copy(g, r).start()

            @pl.when(ang == first_owner + g * nr + r)
            def _():
                pltpu.make_async_copy(
                    swept.at[g, :, 8 * r : 8 * r + 8], planes.at[ang], plane_recv
                ).start()

    def zone_copies():
        order = ang - first_owner
        copies = []
        for side, target in ((0, 0), (1, n_ang - 1)):
            copies.append(
                pltpu.make_async_remote_copy(
                    src_ref=theta_out.at[side],
                    dst_ref=theta_in.at[order],
                    send_sem=zone_send.at[n_ang + side],
                    recv_sem=theta_recv,
                    device_id=(twin, rad, target),
                    device_id_type=MESH,
                )
            )
        for target in range(n_ang):
            copies.append(
                pltpu.make_async_remote_copy(
                    src_ref=phi_out.at[target // (n_ang // 2)],
                    dst_ref=phi_in.at[order],
                    send_sem=zone_send.at[target],
                    recv_sem=phi_recv,
                    device_id=(twin, rad, target),
                    device_id_type=MESH,
                )
            )
        return copies

    @pl.when(is_owner)
    def _():
        pltpu.make_async_copy(planes, planes, plane_recv).wait()
        cells = 2 * theta_cells
        x = jnp.concatenate(
            [planes[:, c].reshape(cells, 128) for c in range(nphi // 128)], axis=1
        )
        for i, part in enumerate((x, pltpu.roll(x, nphi - 1, 1))):
            high = part.astype(BF16)
            split[i * cells : (i + 1) * cells, 0:nphi] = high
            split[i * cells : (i + 1) * cells, nphi : 2 * nphi] = (
                part - high.astype(F32)
            ).astype(BF16)
        x = split[...]
        for z in range(0, zones, 256):
            y = jnp.dot(x, onehot[:, z : z + 256], preferred_element_type=F32)
            picked = (
                near_weight[:, z : z + 256] * y[:cells] + far_weight[:, z : z + 256] * y[cells:]
            )
            zone_sum[:, z : z + 256] = picked.reshape(n_ang, 2 * nt, 256).sum(axis=0)
        for f in range(2):
            line = jnp.sum(zone_sum[f * nt : (f + 1) * nt, :], axis=0, keepdims=True)
            for side in range(2):
                for row in range(G):
                    start = (side * G + row) * nphi
                    theta_out[side, row, f : f + 1, :] = line[:, start : start + nphi]
                start = 2 * G * nphi + side * 128
                phi_out[side, f : f + 1, :] = line[:, start : start + 128]
        for copy in zone_copies():
            copy.start()

    pltpu.make_async_copy(phi_in, phi_in, phi_recv).wait()
    for g in range(groups):
        for r in range(nr):
            @pl.when(ang != first_owner + g * nr + r)
            def _():
                plane_copy(g, r).wait_send()

    for o in range(owners):
        phi_rows[2 * o : 2 * o + 2, :] = phi_in[o]
    rows = phi_rows[...]
    lane = lax.broadcasted_iota(jnp.int32, (8, 128), 1)
    start = lax.rem(ang, n_ang // 2) * (2 * G * nt)
    for t in range(nt):
        left = pltpu.roll(rows, lax.rem(256 - start - 2 * G * t, 128), 1)
        right = pltpu.roll(rows, lax.rem(256 - start - 2 * G * t - 2 * G, 128), 1)
        for g in range(groups):
            line = get(swept, g, pl.ds(t, 2 * nr, stride=nt))
            line = jnp.concatenate(
                [
                    jnp.where(lane < G, left[8 * g : 8 * g + 8], line[:, :128]),
                    line[:, 128 : nphi - 128],
                    jnp.where(lane >= 128 - G, right[8 * g : 8 * g + 8], line[:, nphi - 128 :]),
                ],
                axis=1,
            )
            put(stage, g, pl.ds(t, 2 * nr, stride=nt), line)

    def fill_rows(first_row):
        pltpu.make_async_copy(theta_in, theta_in, theta_recv).wait()
        for row in range(G):
            for g in range(groups):
                for r in range(nr):
                    ang_ext[g, row, 2 * r : 2 * r + 2, :] = theta_in[g * nr + r, row]
                put(stage, g, pl.ds(first_row + row, 2 * nr, stride=nt), ang_ext[g, row])

    @pl.when(ang == 0)
    def _():
        fill_rows(0)

    @pl.when(ang == n_ang - 1)
    def _():
        fill_rows(nt - G)

    for g in range(groups):
        for f in range(2):
            for r in range(nr):
                row = (2 * r + f) * nt
                out_ref[2 * g + f, r] = get(stage, g, pl.ds(row, nt))

    for copy in rad_vel_copies + ang_vel_copies:
        copy.wait_send()
    for g in range(groups):
        for copy in rad_copies[g] + ang_copies[g]:
            copy.wait_send()

    @pl.when(is_owner)
    def _():
        for copy in zone_copies():
            copy.wait_send()


def solution(mesh):
    n_rad, n_ang = mesh.shape["rad"], mesh.shape["ang"]

    def body(state, velocity, band_donor, band_weight):
        _, fields, nr, nt, nphi = state.shape
        zones = band_donor.shape[1]
        groups = fields // 2
        owners = groups * nr
        theta_cells = nt * n_ang
        sizes = (n_rad, n_ang, groups, nr, nt, nphi, theta_cells, zones)
        n_halo = 4 * groups + 4
        out = pl.pallas_call(
            functools.partial(kernel, sizes),
            out_shape=jax.ShapeDtypeStruct((fields, nr, nt, nphi), F32),
            in_specs=[
                pl.BlockSpec(memory_space=pl.ANY),
                pl.BlockSpec(memory_space=pl.ANY),
                pl.BlockSpec(memory_space=pltpu.VMEM),
                pl.BlockSpec(memory_space=pltpu.VMEM),
            ],
            out_specs=pl.BlockSpec(memory_space=pltpu.VMEM),
            scratch_shapes=[
                pltpu.VMEM((fields, nr, nt, nphi), F32),
                pltpu.VMEM((3, nr, nt, nphi), F32),
                pltpu.VMEM((groups, nr + 6, 8, nphi), F32),
                pltpu.VMEM((nr + 2, 8, nphi), F32),
                pltpu.VMEM((groups + 2, nphi // 128, 8 * nr, 128), F32),
                pltpu.VMEM((groups, nt + 6, 8, nphi), F32),
                pltpu.VMEM((nt + 2, 8, nphi), F32),
                pltpu.VMEM((3, 8 * nt, nphi + 128), F32),
                pltpu.VMEM((groups, nphi // 128, 8 * nr, 128), F32),
                pltpu.VMEM((n_ang, nphi // 128, 2 * nt, 128), F32),
                pltpu.VMEM((4 * theta_cells, 2 * nphi), BF16),
                pltpu.VMEM((2 * nphi, zones), BF16),
                pltpu.VMEM((2 * theta_cells, zones), F32),
                pltpu.VMEM((2 * theta_cells, zones), F32),
                pltpu.VMEM((2 * nt, zones), F32),
                pltpu.VMEM((2, G, 2, nphi), F32),
                pltpu.VMEM((2, 2, 128), F32),
                pltpu.VMEM((owners, G, 2, nphi), F32),
                pltpu.VMEM((owners, 2, 128), F32),
                pltpu.VMEM((2 * owners, 128), F32),
                pltpu.SemaphoreType.DMA((2,)),
                pltpu.SemaphoreType.DMA((n_halo,)),
                pltpu.SemaphoreType.DMA((n_halo,)),
                pltpu.SemaphoreType.DMA((owners,)),
                pltpu.SemaphoreType.DMA,
                pltpu.SemaphoreType.DMA((n_ang + 2,)),
                pltpu.SemaphoreType.DMA,
                pltpu.SemaphoreType.DMA,
            ],
            compiler_params=pltpu.CompilerParams(
                collective_id=0, has_side_effects=True, vmem_limit_bytes=40 * 1024 * 1024
            ),
        )(state[0], velocity[0], band_donor, band_weight)
        return out[None]

    spec = P("panel", None, "rad", "ang", None)
    return jax.shard_map(
        body, mesh=mesh, in_specs=(spec, spec, P(), P()), out_specs=spec, check_vma=False
    )
```

time: 478 us -> 54.5 us (0.11)
  the two profiles are of different devices: /device:TPU:40 before, /device:TPU:1 now
where the time goes in v1:
time: 54.5 us; the launch traced here: 54.2 us
  Pallas kernels  50.2 us (92%)
  local copies, waits for them, and re-layouts  3.99 us (7%)
    pallas_call x1, Pallas kernels, body(): pl.pallas_call(functools.partial(kernel, sizes), out_shape=jax.ShapeDtype...  50.2 us
    unnamed x9, local copies, waits for them, and re-layouts  3.99 us

profile of v1, /device:TPU:1, one launch (start us, length us, event | category | flops | bytes accessed | tf_op | source)
XLA Modules:
  0.0 54.2 jit_solution(16373198846183778837)
XLA Ops:
  0.0 0.0 copy-start
  0.0 0.9 %copy-done = f32[1,6,4,4,384]{4,3,2,1,0:T(4,128)S(1)} copy-done((f32[1,6,4,4,384]{4,3,2,1,0:T(4,128)S(1)}, f32[1,6,4,4,384]{4,3,2,1,0:T(4,128)}, u32[]{:S(2)}) %copy-start) | copy-done | bytes 147480
  0.9 0.0 copy-start.1
  0.9 0.9 %copy-done.1 = f32[1,3,4,4,384]{4,3,2,1,0:T(4,128)S(1)} copy-done((f32[1,3,4,4,384]{4,3,2,1,0:T(4,128)S(1)}, f32[1,3,4,4,384]{4,3,2,1,0:T(4,128)}, u32[]{:S(2)}) %copy-start.1) | copy-done | bytes 73752
  1.8 0.0 copy-start.2
  1.8 0.8 %copy-done.2 = f32[2,4,1792]{2,1,0:T(4,128)S(1)} copy-done((f32[2,4,1792]{2,1,0:T(4,128)S(1)}, f32[2,4,1792]{2,1,0:T(4,128)}, u32[]{:S(2)}) %copy-start.2) | copy-done | bytes 57368
  2.6 0.0 copy-start.3
  2.6 0.7 %copy-done.3 = s32[2,1792]{1,0:T(2,128)S(1)} copy-done((s32[2,1792]{1,0:T(2,128)S(1)}, s32[2,1792]{1,0:T(2,128)}, u32[]{:S(2)}) %copy-start.3) | copy-done | bytes 14360
  3.3 50.2 %shard_map.46 = f32[6,4,4,384]{3,2,1,0:T(4,128)S(1)} custom-call(f32[6,4,4,384]{3,2,1,0:T(4,128)S(1)} %bitcast.4, f32[3,4,4,384]{3,2,1,0:T(4,128)S(1)} %bitcast.5, s32[2,1792]{1,0:T(2,128)S(1)} %copy-done.3, f32[2,4,1792]{2,1,0:T(4,128)S(1)} %copy-done.2), custom_call_target="tpu_custom_call" | custom-call | tf_op jit(solution)/shard_map/pallas_call | solution.py:484
  53.6 0.7 %copy.6 = f32[1,6,4,4,384]{4,3,2,1,0:T(4,128)} copy(f32[1,6,4,4,384]{4,3,2,1,0:T(4,128)S(1)} %bitcast.3) | data formatting | bytes 294912
Async XLA Ops:
  0.0 0.9 %copy-start = (f32[1,6,4,4,384]{4,3,2,1,0:T(4,128)S(1)}, f32[1,6,4,4,384]{4,3,2,1,0:T(4,128)}, u32[]{:S(2)}) copy-start(f32[1,6,4,4,384]{4,3,2,1,0:T(4,128)} %param.4) | copy-start | bytes 442372
  0.9 0.9 %copy-start.1 = (f32[1,3,4,4,384]{4,3,2,1,0:T(4,128)S(1)}, f32[1,3,4,4,384]{4,3,2,1,0:T(4,128)}, u32[]{:S(2)}) copy-start(f32[1,3,4,4,384]{4,3,2,1,0:T(4,128)} %param.5) | copy-start | bytes 221188
  1.8 0.8 %copy-start.2 = (f32[2,4,1792]{2,1,0:T(4,128)S(1)}, f32[2,4,1792]{2,1,0:T(4,128)}, u32[]{:S(2)}) copy-start(f32[2,4,1792]{2,1,0:T(4,128)} %weight_ref.1) | copy-start | bytes 172036
  2.6 0.7 %copy-start.3 = (s32[2,1792]{1,0:T(2,128)S(1)}, s32[2,1792]{1,0:T(2,128)}, u32[]{:S(2)}) copy-start(s32[2,1792]{1,0:T(2,128)} %donor_ref.1) | copy-start | bytes 43012

commit v2 on v1

--- a/solution.py
+++ b/solution.py
@@ -94,11 +94,13 @@
     sizes,
     state_hbm,
     velocity_hbm,
-    donor_ref,
-    weight_ref,
+    donor_hbm,
+    weight_hbm,
     out_ref,
     own,
     vel,
+    donor_ref,
+    weight_ref,
     rad_ext,
     rad_vel,
     stage,
@@ -125,6 +127,7 @@
     zone_send,
     theta_recv,
     phi_recv,
+    token_sem,
 ):
     n_rad, n_ang, groups, nr, nt, nphi, theta_cells, zones = sizes
     panel = lax.axis_index("panel")
@@ -138,31 +141,28 @@
 
     load_state = pltpu.make_async_copy(state_hbm, own, local_sem.at[0])
     load_velocity = pltpu.make_async_copy(velocity_hbm, vel, local_sem.at[1])
-    load_state.start()
-    load_velocity.start()
-
-    rad_down = (panel, lax.rem(rad + n_rad - 1, n_rad), ang)
-    rad_up = (panel, lax.rem(rad + 1, n_rad), ang)
-    ang_down = (panel, rad, lax.rem(ang + n_ang - 1, n_ang))
-    ang_up = (panel, rad, lax.rem(ang + 1, n_ang))
+    load_donor = pltpu.make_async_copy(donor_hbm, donor_ref, local_sem.at[2])
+    load_weight = pltpu.make_async_copy(weight_hbm, weight_ref, local_sem.at[3])
+    for load in (load_state, load_velocity, load_donor, load_weight):
+        load.start()
+
+    rad_down, rad_up = (panel, rad - 1, ang), (panel, rad + 1, ang)
+    ang_down, ang_up = (panel, rad, ang - 1), (panel, rad, ang + 1)
+    has_rad = (rad > 0, rad < n_rad - 1)
+    has_ang = (ang > 0, ang < n_ang - 1)
 
     barrier = pltpu.get_barrier_semaphore()
-    pl.semaphore_signal(barrier, inc=1, device_id=rad_down, device_id_type=MESH)
-    pl.semaphore_signal(barrier, inc=1, device_id=rad_up, device_id_type=MESH)
-    members = 2 * n_ang
-    place = panel * n_ang + ang
-
-    def greet(k, carry):
-        other = lax.rem(place + k, members)
-        pl.semaphore_signal(
-            barrier,
-            inc=1,
-            device_id=(other // n_ang, rad, lax.rem(other, n_ang)),
-            device_id_type=MESH,
-        )
-        return carry
-
-    lax.fori_loop(1, members, greet, 0)
+    for exists, device in zip(has_rad, (rad_down, rad_up)):
+
+        @pl.when(exists)
+        def _():
+            pl.semaphore_signal(barrier, inc=1, device_id=device, device_id_type=MESH)
+
+    def ring(distance):
+        return (panel, rad, lax.rem(ang + distance + n_ang, n_ang))
+
+    for device in (ring(-1), ring(1), (twin, rad, ang)):
+        pl.semaphore_signal(barrier, inc=1, device_id=device, device_id_type=MESH)
 
     load_state.wait()
     load_velocity.wait()
@@ -179,7 +179,37 @@
     for t in range(nt):
         ang_vel[1 + t] = get(stage, groups, pl.ds(t, 2 * nr, stride=nt))
 
-    pl.semaphore_wait(barrier, members + 1)
+    def edges(has, fills):
+        for exists, fill in zip(has, fills):
+            pl.when(jnp.logical_not(exists))(fill)
+
+    def fill_rad(source, ends, buffers):
+        def fill():
+            rad_vel[ends[1]] = rad_vel[source]
+            for g in range(groups):
+                for i in buffers:
+                    rad_ext[g, i] = rad_ext[g, source + 2]
+
+        return fill
+
+    def fill_ang_vel(source, end):
+        def fill():
+            ang_vel[end] = ang_vel[source]
+
+        return fill
+
+    edges(
+        has_rad,
+        (
+            fill_rad(1, (1, 0), range(3)),
+            fill_rad(nr, (nr, nr + 1), range(nr + 3, nr + 6)),
+        ),
+    )
+    edges(has_ang, (fill_ang_vel(1, 0), fill_ang_vel(nt, nt + 1)))
+
+    pl.semaphore_wait(
+        barrier, 3 + jnp.where(rad > 0, 1, 0) + jnp.where(rad < n_rad - 1, 1, 0)
+    )
 
     def send(src, dst, slot, device):
         return pltpu.make_async_remote_copy(
@@ -191,34 +221,64 @@
             device_id_type=MESH,
         )
 
-    rad_copies, ang_copies = [], []
-    for g in range(groups):
-        rad_copies.append(
-            (
-                send(rad_ext.at[g, 3:6], rad_ext.at[g, nr + 3 : nr + 6], 4 * g, rad_down),
-                send(rad_ext.at[g, nr : nr + 3], rad_ext.at[g, 0:3], 4 * g + 1, rad_up),
-            )
+    def both(has, pair, act):
+        down, up = pair
+
+        @pl.when(has[0])
+        def _():
+            act(down, up)
+
+        @pl.when(has[1])
+        def _():
+            act(up, down)
+
+    def start(mine, theirs):
+        mine().start()
+
+    def wait_send(mine, theirs):
+        mine().wait_send()
+
+    def wait_recv(mine, theirs):
+        theirs().wait_recv()
+
+    def rad_copies(g):
+        return (
+            lambda: send(rad_ext.at[g, 3:6], rad_ext.at[g, nr + 3 : nr + 6], 4 * g, rad_down),
+            lambda: send(rad_ext.at[g, nr : nr + 3], rad_ext.at[g, 0:3], 4 * g + 1, rad_up),
         )
-        ang_copies.append(
-            (
-                send(ang_ext.at[g, 3:6], ang_ext.at[g, nt + 3 : nt + 6], 4 * g + 2, ang_down),
-                send(ang_ext.at[g, nt : nt + 3], ang_ext.at[g, 0:3], 4 * g + 3, ang_up),
-            )
+
+    def ang_copies(g):
+        return (
+            lambda: send(ang_ext.at[g, 3:6], ang_ext.at[g, nt + 3 : nt + 6], 4 * g + 2, ang_down),
+            lambda: send(ang_ext.at[g, nt : nt + 3], ang_ext.at[g, 0:3], 4 * g + 3, ang_up),
         )
+
     base = 4 * groups
     rad_vel_copies = (
-        send(rad_vel.at[1], rad_vel.at[nr + 1], base, rad_down),
-        send(rad_vel.at[nr], rad_vel.at[0], base + 1, rad_up),
+        lambda: send(rad_vel.at[1], rad_vel.at[nr + 1], base, rad_down),
+        lambda: send(rad_vel.at[nr], rad_vel.at[0], base + 1, rad_up),
     )
     ang_vel_copies = (
-        send(ang_vel.at[1], ang_vel.at[nt + 1], base + 2, ang_down),
-        send(ang_vel.at[nt], ang_vel.at[0], base + 3, ang_up),
-    )
-    for copy in rad_vel_copies + rad_copies[0] + ang_vel_copies:
-        copy.start()
-    for g in range(1, groups):
-        for copy in rad_copies[g]:
-            copy.start()
+        lambda: send(ang_vel.at[1], ang_vel.at[nt + 1], base + 2, ang_down),
+        lambda: send(ang_vel.at[nt], ang_vel.at[0], base + 3, ang_up),
+    )
+    both(has_rad, rad_vel_copies, start)
+    for g in range(groups):
+        both(has_rad, rad_copies(g), start)
+    both(has_ang, ang_vel_copies, start)
+
+    def tell(level):
+        for distance in (-(2**level), 2**level):
+            pl.semaphore_signal(
+                token_sem.at[level], inc=1, device_id=ring(distance), device_id_type=MESH
+            )
+
+    def hear(level):
+        pl.semaphore_wait(token_sem.at[level], 2)
+
+    tell(0)
+    load_donor.wait()
+    load_weight.wait()
 
     @pl.when(is_owner)
     def _():
@@ -246,6 +306,9 @@
             onehot[0:nphi, z : z + 128] = hot
             onehot[nphi : 2 * nphi, z : z + 128] = hot
 
+    hear(0)
+    tell(1)
+
     def wide(x, tiles):
         return jnp.concatenate([x] * tiles, axis=-1)
 
@@ -271,12 +334,11 @@
         azi_coef[i] = coefficient
     azimuth_rate = wide(azimuth_rate, tiles)
 
-    for copy in rad_vel_copies:
-        copy.wait_recv()
+    hear(1)
+    tell(2)
+
+    both(has_rad, rad_vel_copies, wait_recv)
     v = rad_vel[...]
-    v_first = jnp.where(rad == 0, v[1:2], v[0:1])
-    v_last = jnp.where(rad == n_rad - 1, v[nr : nr + 1], v[nr + 1 : nr + 2])
-    v = jnp.concatenate([v_first, v[1 : nr + 1], v_last], axis=0)
     radius_face = INNER_RADIUS + (rad * nr + lead(nr + 1)).astype(F32) * radius_step
     radius_cell = INNER_RADIUS + ((rad * nr + lead(nr)).astype(F32) + 0.5) * radius_step
     rad_coef = flux_coefficients(
@@ -286,28 +348,28 @@
     )
     rad_rate = wide(time_step / (radius_cell * radius_cell * radius_step), tiles)
     for g in range(groups):
-        for copy in rad_copies[g]:
-            copy.wait_recv()
-        q = rad_ext[g]
-        inner = q[3 : nr + 3]
-        low = jnp.where(rad == 0, jnp.concatenate([inner[0:1]] * 3, axis=0), q[0:3])
-        high = jnp.where(
-            rad == n_rad - 1, jnp.concatenate([inner[nr - 1 : nr]] * 3, axis=0), q[nr + 3 : nr + 6]
-        )
-        after = sweep_leading(jnp.concatenate([low, inner, high], axis=0), *rad_coef, rad_rate)
+        both(has_rad, rad_copies(g), wait_recv)
+        after = sweep_leading(rad_ext[g], *rad_coef, rad_rate)
         for r in range(nr):
             put(stage, g, pl.ds(8 * r, 8), after[r])
         for t in range(nt):
             ang_ext[g, 3 + t] = get(stage, g, pl.ds(t, 2 * nr, stride=nt))
-        for copy in ang_copies[g]:
-            copy.start()
-
-    for copy in ang_vel_copies:
-        copy.wait_recv()
+        both(has_ang, ang_copies(g), start)
+
+        def fill_ang(source, targets):
+            def fill():
+                for i in targets:
+                    ang_ext[g, i] = ang_ext[g, source]
+
+            return fill
+
+        edges(
+            has_ang,
+            (fill_ang(3, range(3)), fill_ang(nt + 2, range(nt + 3, nt + 6))),
+        )
+
+    both(has_ang, ang_vel_copies, wait_recv)
     v = ang_vel[...]
-    v_first = jnp.where(ang == 0, v[1:2], v[0:1])
-    v_last = jnp.where(ang == n_ang - 1, v[nt : nt + 1], v[nt + 1 : nt + 2])
-    v = jnp.concatenate([v_first, v[1 : nt + 1], v_last], axis=0)
     theta_face = theta_start + (ang * nt + lead(nt + 1)).astype(F32) * theta_step
     radius_of_face = INNER_RADIUS + ((rad * nr + sub(nt + 1) // 2).astype(F32) + 0.5) * radius_step
     ang_coef = flux_coefficients(
@@ -326,16 +388,10 @@
             device_id_type=MESH,
         )
 
-    for g in range(groups):
-        for copy in ang_copies[g]:
-            copy.wait_recv()
-        q = ang_ext[g]
-        inner = q[3 : nt + 3]
-        low = jnp.where(ang == 0, jnp.concatenate([inner[0:1]] * 3, axis=0), q[0:3])
-        high = jnp.where(
-            ang == n_ang - 1, jnp.concatenate([inner[nt - 1 : nt]] * 3, axis=0), q[nt + 3 : nt + 6]
-        )
-        polar = sweep_leading(jnp.concatenate([low, inner, high], axis=0), *ang_coef, polar_rate)
+    hear(2)
+    for g in range(groups):
+        both(has_ang, ang_copies(g), wait_recv)
+        polar = sweep_leading(ang_ext[g], *ang_coef, polar_rate)
         cells = with_ghost_lanes(polar.reshape(nt * 8, nphi))
         done = sweep_lanes(cells, azi_coef[0], azi_coef[1], azi_coef[2], azimuth_rate)
         for t in range(nt):
@@ -458,11 +514,11 @@
                 row = (2 * r + f) * nt
                 out_ref[2 * g + f, r] = get(stage, g, pl.ds(row, nt))
 
-    for copy in rad_vel_copies + ang_vel_copies:
-        copy.wait_send()
-    for g in range(groups):
-        for copy in rad_copies[g] + ang_copies[g]:
-            copy.wait_send()
+    both(has_rad, rad_vel_copies, wait_send)
+    both(has_ang, ang_vel_copies, wait_send)
+    for g in range(groups):
+        both(has_rad, rad_copies(g), wait_send)
+        both(has_ang, ang_copies(g), wait_send)
 
     @pl.when(is_owner)
     def _():
@@ -484,16 +540,13 @@
         out = pl.pallas_call(
             functools.partial(kernel, sizes),
             out_shape=jax.ShapeDtypeStruct((fields, nr, nt, nphi), F32),
-            in_specs=[
-                pl.BlockSpec(memory_space=pl.ANY),
-                pl.BlockSpec(memory_space=pl.ANY),
-                pl.BlockSpec(memory_space=pltpu.VMEM),
-                pl.BlockSpec(memory_space=pltpu.VMEM),
-            ],
+            in_specs=[pl.BlockSpec(memory_space=pltpu.HBM)] * 4,
             out_specs=pl.BlockSpec(memory_space=pltpu.VMEM),
             scratch_shapes=[
                 pltpu.VMEM((fields, nr, nt, nphi), F32),
                 pltpu.VMEM((3, nr, nt, nphi), F32),
+                pltpu.VMEM((2, zones), jnp.int32),
+                pltpu.VMEM((2, 4, zones), F32),
                 pltpu.VMEM((groups, nr + 6, 8, nphi), F32),
                 pltpu.VMEM((nr + 2, 8, nphi), F32),
                 pltpu.VMEM((groups + 2, nphi // 128, 8 * nr, 128), F32),
@@ -512,7 +565,7 @@
                 pltpu.VMEM((owners, G, 2, nphi), F32),
                 pltpu.VMEM((owners, 2, 128), F32),
                 pltpu.VMEM((2 * owners, 128), F32),
-                pltpu.SemaphoreType.DMA((2,)),
+                pltpu.SemaphoreType.DMA((4,)),
                 pltpu.SemaphoreType.DMA((n_halo,)),
                 pltpu.SemaphoreType.DMA((n_halo,)),
                 pltpu.SemaphoreType.DMA((owners,)),
@@ -520,9 +573,10 @@
                 pltpu.SemaphoreType.DMA((n_ang + 2,)),
                 pltpu.SemaphoreType.DMA,
                 pltpu.SemaphoreType.DMA,
+                pltpu.SemaphoreType.REGULAR((3,)),
             ],
             compiler_params=pltpu.CompilerParams(
-                collective_id=0, has_side_effects=True, vmem_limit_bytes=40 * 1024 * 1024
+                collective_id=0, has_side_effects=True, vmem_limit_bytes=64 * 1024 * 1024
             ),
         )(state[0], velocity[0], band_donor, band_weight)
         return out[None]

time: 54.5 us -> 47.1 us (0.86)
  the two profiles are of different devices: /device:TPU:1 before, /device:TPU:9 now
where the time goes in v2:
time: 47.1 us; the launch traced here: 46.9 us
  Pallas kernels  45.3 us (96%)
  local copies, waits for them, and re-layouts  1.59 us (3%)
    pallas_call x1, Pallas kernels, body(): pl.pallas_call(functools.partial(kernel, sizes), out_shape=jax.ShapeDtype...  45.3 us
    unnamed x1, local copies, waits for them, and re-layouts  1.59 us

profile of v2, /device:TPU:9, one launch (start us, length us, event | category | flops | bytes accessed | tf_op | source)
XLA Modules:
  0.0 46.9 jit_solution(16171576055754539550)
XLA Ops:
  0.0 45.3 %shard_map.46 = f32[6,4,4,384]{3,2,1,0:T(4,128)} custom-call(f32[6,4,4,384]{3,2,1,0:T(4,128)} %bitcast.4, f32[3,4,4,384]{3,2,1,0:T(4,128)} %bitcast.5, s32[2,1792]{1,0:T(2,128)} %donor_hbm.1, f32[2,4,1792]{2,1,0:T(4,128)} %weight_hbm.1), custom_call_target="tpu_custom_call" | custom-call | tf_op jit(solution)/shard_map/pallas_call | solution.py:540
  45.3 1.6 %copy.6 = f32[1,6,4,4,384]{4,3,2,1,0:T(4,128)} copy(f32[1,6,4,4,384]{4,3,2,1,0:T(4,128)} %bitcast.3) | data formatting | bytes 294912

commit v3 on v2

v3 whole, which is shorter than its diff:
```python
import functools
import math

import jax
import jax.numpy as jnp
from jax import lax
from jax.experimental import pallas as pl
from jax.experimental.pallas import tpu as pltpu
from jax.sharding import PartitionSpec as P

G = 2
INNER_RADIUS = 1.0
COURANT = 0.8
MESH = pl.DeviceIdType.MESH
F32 = jnp.float32
BF16 = jnp.bfloat16


def geometry(theta_cells, phi_cells):
    theta_step = math.pi / 2 / (theta_cells - 2 * G)
    phi_step = 1.5 * math.pi / (phi_cells - 2 * G)
    radius_step = INNER_RADIUS * theta_step
    theta_start = math.pi / 4 - G * theta_step
    time_step = COURANT * INNER_RADIUS * min(theta_step, math.sin(theta_start) * phi_step)
    return theta_step, phi_step, radius_step, theta_start, time_step


def flux_coefficients(face_speed, area, face_rate):
    size = jnp.abs(face_speed)
    courant = size * face_rate
    half = 0.5 * courant
    a0 = face_speed if area is None else area * face_speed
    a1 = a0 * (half * (1.0 - 2.0 / 3.0 * courant))
    a2 = -(half * (size if area is None else area * size))
    return a0, a1, a2


def clipped_interface(before, left, right, after):
    value = 7.0 / 12.0 * (left + right) - 1.0 / 12.0 * (before + after)
    return jnp.minimum(jnp.maximum(value, jnp.minimum(left, right)), jnp.maximum(left, right))


def sweep_leading(q, a0, a1, a2, rate):
    n = q.shape[0] - 6
    face = clipped_interface(q[0 : n + 3], q[1 : n + 4], q[2 : n + 5], q[3 : n + 6])
    left, right = face[0 : n + 2], face[1 : n + 3]
    spread = right - left
    curvature = 6.0 * (q[2 : n + 4] - 0.5 * (left + right))
    up = a0 > 0
    flux = (
        a0 * face[1 : n + 2]
        + a1 * jnp.where(up, curvature[0 : n + 1], curvature[1 : n + 2])
        + a2 * jnp.where(up, spread[0 : n + 1], spread[1 : n + 2])
    )
    return q[3 : n + 3] - rate * (flux[1 : n + 1] - flux[0:n])


def with_ghost_lanes(x):
    rows, cells = x.shape
    lane = lax.broadcasted_iota(jnp.int32, (rows, 128), 1)
    last = jnp.broadcast_to(x[:, cells - 1 : cells], (rows, 128))
    first = jnp.broadcast_to(x[:, 0:1], (rows, 128))
    return jnp.concatenate([x, jnp.where(lane < 64, last, first)], axis=1)


def sweep_rolled(q, a0, a1, a2, axis):
    width = q.shape[axis]

    def ahead(x):
        return pltpu.roll(x, width - 1, axis)

    def behind(x):
        return pltpu.roll(x, 1, axis)

    face = clipped_interface(pltpu.roll(q, 2, axis), behind(q), q, ahead(q))
    right = ahead(face)
    spread = right - face
    curvature = 6.0 * (q - 0.5 * (face + right))
    up = a0 > 0
    flux = (
        a0 * face
        + a1 * jnp.where(up, behind(curvature), curvature)
        + a2 * jnp.where(up, behind(spread), spread)
    )
    return ahead(flux) - flux


def put(ref, index, rows, value):
    for c in range(value.shape[1] // 128):
        ref[index, c, rows, :] = value[:, 128 * c : 128 * c + 128]


def kernel(
    sizes,
    state_hbm,
    velocity_hbm,
    donor_hbm,
    weight_hbm,
    out_ref,
    own,
    vel,
    donor_ref,
    weight_ref,
    rad_ext,
    rad_vel,
    halo,
    halo_vel,
    stage,
    planes,
    planes_vel,
    block_vel,
    polar_coef,
    azimuth_coef,
    block,
    split,
    onehot,
    near_weight,
    far_weight,
    zone_sum,
    zone_out,
    theta_in,
    phi_in,
    back_out,
    result,
    local_sem,
    halo_send,
    halo_recv,
    plane_send,
    plane_recv,
    zone_send,
    theta_recv,
    phi_recv,
    back_send,
    back_recv,
    token_sem,
):
    n_rad, n_ang, groups, nr, nt, nphi, theta_cells, zones = sizes
    panel = lax.axis_index("panel")
    rad = lax.axis_index("rad")
    ang = lax.axis_index("ang")
    twin = 1 - panel
    theta_step, phi_step, radius_step, theta_start, time_step = geometry(theta_cells, nphi)
    row_index, member = ang // nr, lax.rem(ang, nr)
    row_cells = nr * nt
    fields = 2 * groups
    tiles = nphi // 128
    theta_tiles = 2 * G * tiles

    load_state = pltpu.make_async_copy(state_hbm, own, local_sem.at[0])
    load_velocity = pltpu.make_async_copy(velocity_hbm, vel, local_sem.at[1])
    load_donor = pltpu.make_async_copy(donor_hbm, donor_ref, local_sem.at[2])
    load_weight = pltpu.make_async_copy(weight_hbm, weight_ref, local_sem.at[3])
    for load in (load_state, load_velocity, load_donor, load_weight):
        load.start()

    rad_down, rad_up = (panel, rad - 1, ang), (panel, rad + 1, ang)
    has_rad = (rad > 0, rad < n_rad - 1)

    barrier = pltpu.get_barrier_semaphore()
    for exists, device in zip(has_rad, (rad_down, rad_up)):

        @pl.when(exists)
        def _():
            pl.semaphore_signal(barrier, inc=1, device_id=device, device_id_type=MESH)

    def ring(distance):
        return (panel, rad, lax.rem(ang + distance + n_ang, n_ang))

    for device in (ring(-1), ring(1), (twin, rad, ang)):
        pl.semaphore_signal(barrier, inc=1, device_id=device, device_id_type=MESH)

    pl.semaphore_wait(
        barrier, 3 + jnp.where(rad > 0, 1, 0) + jnp.where(rad < n_rad - 1, 1, 0)
    )

    def send(src, dst, slot, device):
        return pltpu.make_async_remote_copy(
            src_ref=src,
            dst_ref=dst,
            send_sem=halo_send.at[slot],
            recv_sem=halo_recv.at[slot],
            device_id=device,
            device_id_type=MESH,
        )

    def both(has, pair, act):
        down, up = pair

        @pl.when(has[0])
        def _():
            act(down, up)

        @pl.when(has[1])
        def _():
            act(up, down)

    def start(mine, theirs):
        mine().start()

    def wait_send(mine, theirs):
        mine().wait_send()

    def wait_recv(mine, theirs):
        theirs().wait_recv()

    def rad_copies(g):
        return (
            lambda: send(state_hbm.at[pl.ds(2 * g, 2), pl.ds(0, 3)], halo.at[g, 1], 2 * g, rad_down),
            lambda: send(
                state_hbm.at[pl.ds(2 * g, 2), pl.ds(nr - 3, 3)], halo.at[g, 0], 2 * g + 1, rad_up
            ),
        )

    base = 2 * groups
    rad_vel_copies = (
        lambda: send(velocity_hbm.at[0, 0], halo_vel.at[1], base, rad_down),
        lambda: send(velocity_hbm.at[0, nr - 1], halo_vel.at[0], base + 1, rad_up),
    )
    both(has_rad, rad_vel_copies, start)
    for g in range(groups):
        both(has_rad, rad_copies(g), start)
    def tell(level):
        for distance in (-(2**level), 2**level):
            pl.semaphore_signal(
                token_sem.at[level], inc=1, device_id=ring(distance), device_id_type=MESH
            )

    def hear(level):
        pl.semaphore_wait(token_sem.at[level], 2)

    tell(0)
    load_state.wait()
    load_velocity.wait()
    for g in range(groups):
        for f in range(2):
            for r in range(nr):
                rad_ext[g, 3 + r, f * nt : (f + 1) * nt, :] = own[2 * g + f, r]
    for r in range(nr):
        for f in range(2):
            rad_vel[1 + r, f * nt : (f + 1) * nt, :] = vel[0, r]

    def edges(has, fills):
        for exists, fill in zip(has, fills):
            pl.when(jnp.logical_not(exists))(fill)

    def fill_rad(source, ends, buffers):
        def fill():
            rad_vel[ends[1]] = rad_vel[source]
            for g in range(groups):
                for i in buffers:
                    rad_ext[g, i] = rad_ext[g, source + 2]

        return fill

    edges(
        has_rad,
        (
            fill_rad(1, (1, 0), range(3)),
            fill_rad(nr, (nr, nr + 1), range(nr + 3, nr + 6)),
        ),
    )


    load_donor.wait()
    load_weight.wait()

    donor_all = donor_ref[...]
    donor = jnp.where(panel == 0, donor_all[1:2], donor_all[0:1]).astype(F32)
    donor_row = jnp.floor((donor + 0.5) * (1.0 / nphi))
    donor_col = donor - donor_row * nphi
    weights = jnp.where(panel == 0, weight_ref[1], weight_ref[0])
    row_of = lax.broadcasted_iota(jnp.int32, (row_cells, 128), 0)
    row_of = (row_index * row_cells + row_of).astype(F32)
    col_of = lax.broadcasted_iota(jnp.int32, (nphi, 128), 0).astype(F32)
    for z in range(0, zones, 128):
        here = donor_row[:, z : z + 128]
        w = weights[:, z : z + 128]
        at_row = row_of == here
        above = row_of == here + 1.0
        near_weight[:, z : z + 128] = jnp.where(at_row, w[0:1], jnp.where(above, w[2:3], 0.0))
        far_weight[:, z : z + 128] = jnp.where(at_row, w[1:2], jnp.where(above, w[3:4], 0.0))
        hot = jnp.where(col_of == donor_col[:, z : z + 128], 1.0, 0.0).astype(BF16)
        onehot[0:nphi, z : z + 128] = hot
        onehot[nphi : 2 * nphi, z : z + 128] = hot

    hear(0)
    tell(1)

    def wide(x, tiles):
        return jnp.concatenate([x] * tiles, axis=-1)

    hear(1)
    tell(2)

    has_block = (row_index > 0, row_index < n_ang // nr - 1)

    def exchange(source, target, sends, recvs):
        def to(other_row, k, slot, send_slot, recv_slot):
            return pltpu.make_async_remote_copy(
                src_ref=source(k),
                dst_ref=target.at[slot],
                send_sem=sends.at[send_slot],
                recv_sem=recvs.at[recv_slot],
                device_id=(panel, rad, other_row * nr + k),
                device_id_type=MESH,
            )

        def all_remote(act):
            for step in range(1, nr):
                act(to(row_index, lax.rem(member + step, nr), member + 1, step, 0))

            @pl.when(has_block[1] & (member == nr - 1))
            def _():
                for k in range(nr):
                    act(to(row_index + 1, k, 0, nr + k, 1))

            @pl.when(has_block[0] & (member == 0))
            def _():
                for k in range(nr):
                    act(to(row_index - 1, k, nr + 1, 2 * nr + k, 2))

        def begin():
            all_remote(lambda copy: copy.start())
            pltpu.make_async_copy(source(member), target.at[member + 1], recvs.at[0]).start()

        def arrive():
            members = target.at[pl.ds(1, nr)]
            pltpu.make_async_copy(members, members, recvs.at[0]).wait()
            for side, slot in ((0, 0), (1, nr + 1)):

                @pl.when(has_block[side])
                def _():
                    edge = target.at[slot]
                    pltpu.make_async_copy(edge, edge, recvs.at[1 + side]).wait()

        def finish():
            all_remote(lambda copy: copy.wait_send())

        return begin, arrive, finish

    vel_begin, vel_arrive, vel_finish = exchange(
        lambda k: velocity_hbm.at[pl.ds(1, 2), k], planes_vel, plane_send.at[0], plane_recv.at[0]
    )
    plane_begin, plane_arrive, plane_finish = exchange(
        lambda k: stage.at[:, :, pl.ds(pl.multiple_of(8 * k, 8), 8)],
        planes,
        plane_send.at[1],
        plane_recv.at[1],
    )
    vel_begin()

    def lead(n):
        return lax.broadcasted_iota(jnp.int32, (n, 8, 128), 0)


    both(has_rad, rad_vel_copies, wait_recv)
    for side, end in ((0, 0), (1, nr + 1)):

        @pl.when(has_rad[side])
        def _():
            for f in range(2):
                rad_vel[end, f * nt : (f + 1) * nt, :] = halo_vel[side]

    v = rad_vel[...]
    radius_face = INNER_RADIUS + (rad * nr + lead(nr + 1)).astype(F32) * radius_step
    radius_cell = INNER_RADIUS + ((rad * nr + lead(nr)).astype(F32) + 0.5) * radius_step
    rad_coef = flux_coefficients(
        0.5 * (v[0 : nr + 1] + v[1 : nr + 2]),
        wide(radius_face * radius_face, tiles),
        time_step / radius_step,
    )
    rad_rate = wide(time_step / (radius_cell * radius_cell * radius_step), tiles)
    for g in range(groups):
        both(has_rad, rad_copies(g), wait_recv)
        for side, first in ((0, 0), (1, nr + 3)):

            @pl.when(has_rad[side])
            def _():
                for f in range(2):
                    for i in range(3):
                        rad_ext[g, first + i, f * nt : (f + 1) * nt, :] = halo[g, side, f, i]

        after = sweep_leading(rad_ext[g], *rad_coef, rad_rate)
        for r in range(nr):
            put(stage, g, pl.ds(8 * r, 8), after[r])
    plane_begin()

    vel_arrive()
    for slot in range(nr + 2):
        block_vel[0, slot * nt : (slot + 1) * nt, :] = planes_vel[slot, 0]
    for slot in range(nr):
        block_vel[1, slot * nt : (slot + 1) * nt, :] = planes_vel[slot + 1, 1]
    ext = row_cells + 2 * nt
    ghosts = ((0, nt, nt), (nt + row_cells, ext, nt + row_cells - 1))

    def fill_ghosts(ref, index):
        for side, (first, last, source) in enumerate(ghosts):

            @pl.when(jnp.logical_not(has_block[side]))
            def _():
                for i in index:
                    ref[i, first:last, :] = jnp.broadcast_to(
                        ref[i, source : source + 1, :], (nt, nphi)
                    )

    fill_ghosts(block_vel, range(1))

    def places(n, first):
        return lax.broadcasted_iota(jnp.int32, (n, 128), 0) + (row_index * row_cells + first)

    def shell_radius(n):
        shell = jnp.zeros((n, 128), jnp.int32) + (rad * nr + member)
        return INNER_RADIUS + (shell.astype(F32) + 0.5) * radius_step

    face_place = places(ext, -nt).astype(F32)
    radius = shell_radius(ext)
    u = block_vel[0, 0:ext, :]
    for i, coefficient in enumerate(
        flux_coefficients(
            0.5 * (u + pltpu.roll(u, 1, 0)),
            wide(jnp.sin(theta_start + face_place * theta_step), tiles),
            wide(time_step / (radius * theta_step), tiles),
        )
    ):
        polar_coef[i] = coefficient
    sin_cell = jnp.sin(theta_start + (face_place + 0.5) * theta_step)
    polar_coef[3] = wide(time_step / (radius * sin_cell * theta_step), tiles)
    sin_cell = jnp.sin(theta_start + (places(row_cells, 0).astype(F32) + 0.5) * theta_step)
    rate = wide(time_step / (shell_radius(row_cells) * sin_cell * phi_step), tiles + 1)
    u = with_ghost_lanes(block_vel[1, 0:row_cells, :])
    for i, coefficient in enumerate(
        flux_coefficients(0.5 * (u + pltpu.roll(u, 1, 1)), None, rate)
    ):
        azimuth_coef[i] = coefficient
    azimuth_coef[3] = rate
    hear(2)
    pl.semaphore_signal(
        token_sem.at[3], inc=1, device_id=(twin, rad, ang), device_id_type=MESH
    )

    plane_arrive()
    for slot in range(nr + 2):
        for g in range(groups):
            for c in range(tiles):
                for f in range(2):
                    block[2 * g + f, slot * nt : (slot + 1) * nt, 128 * c : 128 * c + 128] = planes[
                        slot, g, c, f * nt : (f + 1) * nt, :
                    ]
    fill_ghosts(block, range(fields))
    cells = fields * row_cells
    for f in range(fields):
        q = block[f]
        change = sweep_rolled(q, polar_coef[0], polar_coef[1], polar_coef[2], 0)
        q = (q - polar_coef[3] * change)[nt : nt + row_cells]
        wide_q = with_ghost_lanes(q)
        change = sweep_rolled(wide_q, azimuth_coef[0], azimuth_coef[1], azimuth_coef[2], 1)
        q = (wide_q - azimuth_coef[3] * change)[:, :nphi]
        for k in range(nr):
            for c in range(tiles):
                back_out[k, c, f * nt : (f + 1) * nt, :] = q[
                    k * nt : (k + 1) * nt, 128 * c : 128 * c + 128
                ]
        for i, part in enumerate((q, pltpu.roll(q, nphi - 1, 1))):
            coarse = part.astype(BF16)
            row = i * cells + f * row_cells
            split[row : row + row_cells, 0:nphi] = coarse
            split[row : row + row_cells, nphi : 2 * nphi] = (part - coarse.astype(F32)).astype(BF16)

    def back_copy(step):
        other = lax.rem(member + step, nr)
        return pltpu.make_async_remote_copy(
            src_ref=back_out.at[other],
            dst_ref=result.at[member],
            send_sem=back_send.at[step],
            recv_sem=back_recv,
            device_id=(panel, rad, row_index * nr + other),
            device_id_type=MESH,
        )

    theta_tiles = 2 * G * tiles

    def zone_copies():
        copies = []
        for side, target in ((0, 0), (1, n_ang - 1)):
            copies.append(
                pltpu.make_async_remote_copy(
                    src_ref=zone_out.at[pl.ds(side * theta_tiles // 2, theta_tiles // 2)],
                    dst_ref=theta_in.at[ang],
                    send_sem=zone_send.at[n_ang + side],
                    recv_sem=theta_recv,
                    device_id=(twin, rad, target),
                    device_id_type=MESH,
                )
            )
        for target in range(n_ang):
            copies.append(
                pltpu.make_async_remote_copy(
                    src_ref=zone_out.at[theta_tiles + target // (n_ang // 2)],
                    dst_ref=phi_in.at[ang],
                    send_sem=zone_send.at[target],
                    recv_sem=phi_recv,
                    device_id=(twin, rad, target),
                    device_id_type=MESH,
                )
            )
        return copies

    x = split[...]
    for z in range(0, zones, 256):
        y = jnp.dot(x, onehot[:, z : z + 256], preferred_element_type=F32)
        near = near_weight[:, z : z + 256].reshape(1, row_cells, 256)
        far = far_weight[:, z : z + 256].reshape(1, row_cells, 256)
        picked = near * y[:cells].reshape(fields, row_cells, 256) + far * y[cells:].reshape(
            fields, row_cells, 256
        )
        picked = picked.reshape(fields, row_cells // 8, 8, 256).sum(axis=1).reshape(8 * fields, 256)
        for half in range(2):
            zone_sum[z // 128 + half] = picked[:, 128 * half : 128 * half + 128]
    for z in range(zones // 128):
        parts = [zone_sum[z, pl.ds(t, fields, stride=8), :] for t in range(8)]
        while len(parts) > 1:
            parts = [a + b for a, b in zip(parts[::2], parts[1::2])]
        zone_out[z, 0:fields, :] = parts[0]
    pl.semaphore_wait(token_sem.at[3], 1)
    for copy in zone_copies():
        copy.start()

    for step in range(1, nr):
        back_copy(step).start()
    pltpu.make_async_copy(back_out.at[member], result.at[member], back_recv).start()

    pltpu.make_async_copy(result, result, back_recv).wait()
    pltpu.make_async_copy(phi_in, phi_in, phi_recv).wait()
    lane = lax.broadcasted_iota(jnp.int32, (fields, 128), 1)
    first_lane = lax.rem(ang, n_ang // 2) * (2 * G * nt)
    for r in range(nr):
        total = phi_in[r, 0:fields, :]
        for k in range(1, n_ang // nr):
            total = total + phi_in[k * nr + r, 0:fields, :]
        for t in range(nt):
            shift = 256 - first_lane - 2 * G * t
            left = pltpu.roll(total, lax.rem(shift, 128), 1)
            right = pltpu.roll(total, lax.rem(shift - 2 * G, 128), 1)
            rows = pl.ds(t, fields, stride=nt)
            result[r, 0, rows, :] = jnp.where(lane < G, left, result[r, 0, rows, :])
            result[r, tiles - 1, rows, :] = jnp.where(
                lane >= 128 - G, right, result[r, tiles - 1, rows, :]
            )

    def fill_rows(first_row):
        pltpu.make_async_copy(theta_in, theta_in, theta_recv).wait()
        for r in range(nr):
            total = theta_in[r, :, 0:fields, :]
            for k in range(1, n_ang // nr):
                total = total + theta_in[k * nr + r, :, 0:fields, :]
            for row in range(G):
                for c in range(tiles):
                    result[r, c, pl.ds(first_row + row, fields, stride=nt), :] = total[
                        row * tiles + c
                    ]

    @pl.when(ang == 0)
    def _():
        fill_rows(0)

    @pl.when(ang == n_ang - 1)
    def _():
        fill_rows(nt - G)

    for f in range(fields):
        for r in range(nr):
            out_ref[f, r] = jnp.concatenate(
                [result[r, c, f * nt : (f + 1) * nt, :] for c in range(tiles)], axis=1
            )

    both(has_rad, rad_vel_copies, wait_send)
    for g in range(groups):
        both(has_rad, rad_copies(g), wait_send)
    vel_finish()
    plane_finish()
    for step in range(1, nr):
        back_copy(step).wait_send()
    for copy in zone_copies():
        copy.wait_send()


def solution(mesh):
    n_rad, n_ang = mesh.shape["rad"], mesh.shape["ang"]

    def body(state, velocity, band_donor, band_weight):
        _, fields, nr, nt, nphi = state.shape
        zones = band_donor.shape[1]
        groups = fields // 2
        theta_cells = nt * n_ang
        sizes = (n_rad, n_ang, groups, nr, nt, nphi, theta_cells, zones)
        n_halo = 2 * groups + 2
        tiles, row_cells = nphi // 128, nr * nt
        ext = row_cells + 2 * nt
        out = pl.pallas_call(
            functools.partial(kernel, sizes),
            out_shape=jax.ShapeDtypeStruct((fields, nr, nt, nphi), F32),
            in_specs=[pl.BlockSpec(memory_space=pltpu.HBM)] * 4,
            out_specs=pl.BlockSpec(memory_space=pltpu.VMEM),
            scratch_shapes=[
                pltpu.VMEM((fields, nr, nt, nphi), F32),
                pltpu.VMEM((3, nr, nt, nphi), F32),
                pltpu.VMEM((2, zones), jnp.int32),
                pltpu.VMEM((2, 4, zones), F32),
                pltpu.VMEM((groups, nr + 6, 8, nphi), F32),
                pltpu.VMEM((nr + 2, 8, nphi), F32),
                pltpu.VMEM((groups, 2, 2, 3, nt, nphi), F32),
                pltpu.VMEM((2, nt, nphi), F32),
                pltpu.VMEM((groups, tiles, 8 * nr, 128), F32),
                pltpu.VMEM((nr + 2, groups, tiles, 8, 128), F32),
                pltpu.VMEM((nr + 2, 2, nt, nphi), F32),
                pltpu.VMEM((2, ext, nphi), F32),
                pltpu.VMEM((4, ext, nphi), F32),
                pltpu.VMEM((4, row_cells, nphi + 128), F32),
                pltpu.VMEM((fields, ext, nphi), F32),
                pltpu.VMEM((2 * fields * row_cells, 2 * nphi), BF16),
                pltpu.VMEM((2 * nphi, zones), BF16),
                pltpu.VMEM((row_cells, zones), F32),
                pltpu.VMEM((row_cells, zones), F32),
                pltpu.VMEM((zones // 128, 8 * fields, 128), F32),
                pltpu.VMEM((zones // 128, 8, 128), F32),
                pltpu.VMEM((n_ang, G * tiles, 8, 128), F32),
                pltpu.VMEM((n_ang, 8, 128), F32),
                pltpu.VMEM((nr, tiles, fields * nt, 128), F32),
                pltpu.VMEM((nr, tiles, fields * nt, 128), F32),
                pltpu.SemaphoreType.DMA((4,)),
                pltpu.SemaphoreType.DMA((n_halo,)),
                pltpu.SemaphoreType.DMA((n_halo,)),
                pltpu.SemaphoreType.DMA((2, 3 * nr)),
                pltpu.SemaphoreType.DMA((2, 3)),
                pltpu.SemaphoreType.DMA((n_ang + 2,)),
                pltpu.SemaphoreType.DMA,
                pltpu.SemaphoreType.DMA,
                pltpu.SemaphoreType.DMA((nr,)),
                pltpu.SemaphoreType.DMA,
                pltpu.SemaphoreType.REGULAR((4,)),
            ],
            compiler_params=pltpu.CompilerParams(
                collective_id=0, has_side_effects=True, vmem_limit_bytes=40 * 1024 * 1024
            ),
        )(
            *(
                pltpu.with_memory_space_constraint(x, pltpu.HBM)
                for x in (state[0], velocity[0], band_donor, band_weight)
            )
        )
        return out[None]

    spec = P("panel", None, "rad", "ang", None)
    return jax.shard_map(
        body, mesh=mesh, in_specs=(spec, spec, P(), P()), out_specs=spec, check_vma=False
    )
```

time: 47.1 us -> 42.9 us (0.911)
  Pallas kernels: 45.3 us -> 42.1 us
  local copies, waits for them, and re-layouts: 1.59 us -> 0.66 us
    pallas_call x1, Pallas kernels: 45.3 us -> 42.1 us  [body(): pl.pallas_call(functools.partial(kernel, sizes), out_shape=jax.ShapeDtype...]
    unnamed x1, local copies, waits for them, and re-layouts: 1.59 us -> 0.66 us
where the time goes in v3:
time: 42.9 us; the launch traced here: 42.8 us
  Pallas kernels  42.1 us (98%)
  local copies, waits for them, and re-layouts  0.66 us (2%)
    pallas_call x1, Pallas kernels, body(): pl.pallas_call(functools.partial(kernel, sizes), out_shape=jax.ShapeDtype...  42.1 us

profile of v3, /device:TPU:9, one launch (start us, length us, event | category | flops | bytes accessed | tf_op | source)
XLA Modules:
  0.0 42.8 jit_solution(16347706559629597624)
XLA Ops:
  0.0 42.1 %shard_map.46 = f32[6,4,4,384]{3,2,1,0:T(4,128)S(1)} custom-call(f32[6,4,4,384]{3,2,1,0:T(4,128)} %bitcast.4, f32[3,4,4,384]{3,2,1,0:T(4,128)} %bitcast.5, s32[2,1792]{1,0:T(2,128)} %donor_hbm.1, f32[2,4,1792]{2,1,0:T(4,128)} %weight_hbm.1), custom_call_target="tpu_custom_call" | custom-call | tf_op jit(solution)/shard_map/pallas_call | solution.py:599
  42.1 0.7 %copy.6 = f32[1,6,4,4,384]{4,3,2,1,0:T(4,128)} copy(f32[1,6,4,4,384]{4,3,2,1,0:T(4,128)S(1)} %bitcast.3) | data formatting | bytes 294912

commit v4 on v3

--- a/solution.py
+++ b/solution.py
@@ -156,22 +156,36 @@
     rad_down, rad_up = (panel, rad - 1, ang), (panel, rad + 1, ang)
     has_rad = (rad > 0, rad < n_rad - 1)
 
+    reach = nr
     barrier = pltpu.get_barrier_semaphore()
-    for exists, device in zip(has_rad, (rad_down, rad_up)):
+
+    def ring(distance, on_panel):
+        return (on_panel, rad, lax.rem(ang + distance + n_ang, n_ang))
+
+    def signal(semaphore, device):
+        pl.semaphore_signal(semaphore, inc=1, device_id=device, device_id_type=MESH)
+
+    for exists, other in zip(has_rad, (rad - 1, rad + 1)):
 
         @pl.when(exists)
         def _():
-            pl.semaphore_signal(barrier, inc=1, device_id=device, device_id_type=MESH)
-
-    def ring(distance):
-        return (panel, rad, lax.rem(ang + distance + n_ang, n_ang))
-
-    for device in (ring(-1), ring(1), (twin, rad, ang)):
-        pl.semaphore_signal(barrier, inc=1, device_id=device, device_id_type=MESH)
-
-    pl.semaphore_wait(
-        barrier, 3 + jnp.where(rad > 0, 1, 0) + jnp.where(rad < n_rad - 1, 1, 0)
-    )
+            signal(barrier, (0, other, ang))
+
+    signal(barrier, (twin, rad, ang))
+    for distance in range(1, reach + 1):
+        signal(barrier, ring(distance, 1))
+        signal(barrier, ring(-distance, 1))
+
+    @pl.when(panel == 0)
+    def _():
+        pl.semaphore_wait(
+            barrier, 1 + jnp.where(rad > 0, 2, 0) + jnp.where(rad < n_rad - 1, 2, 0)
+        )
+        signal(token_sem.at[0], (twin, rad, ang))
+
+    @pl.when(panel == 1)
+    def _():
+        pl.semaphore_wait(token_sem.at[0], 1)
 
     def send(src, dst, slot, device):
         return pltpu.make_async_remote_copy(
@@ -186,13 +200,13 @@
     def both(has, pair, act):
         down, up = pair
 
+        @pl.when(has[1])
+        def _():
+            act(up, down)
+
         @pl.when(has[0])
         def _():
             act(down, up)
-
-        @pl.when(has[1])
-        def _():
-            act(up, down)
 
     def start(mine, theirs):
         mine().start()
@@ -219,16 +233,82 @@
     both(has_rad, rad_vel_copies, start)
     for g in range(groups):
         both(has_rad, rad_copies(g), start)
-    def tell(level):
-        for distance in (-(2**level), 2**level):
-            pl.semaphore_signal(
-                token_sem.at[level], inc=1, device_id=ring(distance), device_id_type=MESH
+    @pl.when(panel == 1)
+    def _():
+        pl.semaphore_wait(barrier, 1 + 4 * reach)
+        signal(token_sem.at[1], (twin, rad, ang))
+
+    @pl.when(panel == 0)
+    def _():
+        pl.semaphore_wait(token_sem.at[1], 1)
+
+    for distance in (-reach, reach):
+        signal(token_sem.at[2], ring(distance, panel))
+
+    has_block = (row_index > 0, row_index < n_ang // nr - 1)
+
+    def exchange(source, target, sends, recvs):
+        def to(other_row, k, slot, send_slot, recv_slot):
+            return pltpu.make_async_remote_copy(
+                src_ref=source(k),
+                dst_ref=target(slot),
+                send_sem=sends.at[send_slot],
+                recv_sem=recvs.at[recv_slot],
+                device_id=(panel, rad, other_row * nr + k),
+                device_id_type=MESH,
             )
 
-    def hear(level):
-        pl.semaphore_wait(token_sem.at[level], 2)
-
-    tell(0)
+        def all_remote(act):
+            for step in range(1, nr):
+                act(to(row_index, lax.rem(member + step, nr), member + 1, step, 0))
+
+            @pl.when(has_block[1] & (member == nr - 1))
+            def _():
+                for k in range(nr):
+                    act(to(row_index + 1, k, 0, nr + k, 1))
+
+            @pl.when(has_block[0] & (member == 0))
+            def _():
+                for k in range(nr):
+                    act(to(row_index - 1, k, nr + 1, 2 * nr + k, 2))
+
+        def begin():
+            all_remote(lambda copy: copy.start())
+            pltpu.make_async_copy(source(member), target(member + 1), recvs.at[0]).start()
+
+        def arrive():
+            members = target(pl.ds(1, nr))
+            pltpu.make_async_copy(members, members, recvs.at[0]).wait()
+            for side, slot in ((0, 0), (1, nr + 1)):
+
+                @pl.when(has_block[side])
+                def _():
+                    edge = target(slot)
+                    pltpu.make_async_copy(edge, edge, recvs.at[1 + side]).wait()
+
+        def finish():
+            all_remote(lambda copy: copy.wait_send())
+
+        return begin, arrive, finish
+
+    vel_begin, vel_arrive, vel_finish = exchange(
+        lambda k: velocity_hbm.at[pl.ds(1, 2), k],
+        lambda slot: planes_vel.at[slot],
+        plane_send.at[groups],
+        plane_recv.at[groups],
+    )
+
+    def plane_exchange(g):
+        return exchange(
+            lambda k: stage.at[g, :, pl.ds(pl.multiple_of(8 * k, 8), 8)],
+            lambda slot: planes.at[slot, g],
+            plane_send.at[g],
+            plane_recv.at[g],
+        )
+
+    plane_exchanges = [plane_exchange(g) for g in range(groups)]
+    vel_begin()
+
     load_state.wait()
     load_velocity.wait()
     for g in range(groups):
@@ -283,71 +363,10 @@
         onehot[0:nphi, z : z + 128] = hot
         onehot[nphi : 2 * nphi, z : z + 128] = hot
 
-    hear(0)
-    tell(1)
 
     def wide(x, tiles):
         return jnp.concatenate([x] * tiles, axis=-1)
 
-    hear(1)
-    tell(2)
-
-    has_block = (row_index > 0, row_index < n_ang // nr - 1)
-
-    def exchange(source, target, sends, recvs):
-        def to(other_row, k, slot, send_slot, recv_slot):
-            return pltpu.make_async_remote_copy(
-                src_ref=source(k),
-                dst_ref=target.at[slot],
-                send_sem=sends.at[send_slot],
-                recv_sem=recvs.at[recv_slot],
-                device_id=(panel, rad, other_row * nr + k),
-                device_id_type=MESH,
-            )
-
-        def all_remote(act):
-            for step in range(1, nr):
-                act(to(row_index, lax.rem(member + step, nr), member + 1, step, 0))
-
-            @pl.when(has_block[1] & (member == nr - 1))
-            def _():
-                for k in range(nr):
-                    act(to(row_index + 1, k, 0, nr + k, 1))
-
-            @pl.when(has_block[0] & (member == 0))
-            def _():
-                for k in range(nr):
-                    act(to(row_index - 1, k, nr + 1, 2 * nr + k, 2))
-
-        def begin():
-            all_remote(lambda copy: copy.start())
-            pltpu.make_async_copy(source(member), target.at[member + 1], recvs.at[0]).start()
-
-        def arrive():
-            members = target.at[pl.ds(1, nr)]
-            pltpu.make_async_copy(members, members, recvs.at[0]).wait()
-            for side, slot in ((0, 0), (1, nr + 1)):
-
-                @pl.when(has_block[side])
-                def _():
-                    edge = target.at[slot]
-                    pltpu.make_async_copy(edge, edge, recvs.at[1 + side]).wait()
-
-        def finish():
-            all_remote(lambda copy: copy.wait_send())
-
-        return begin, arrive, finish
-
-    vel_begin, vel_arrive, vel_finish = exchange(
-        lambda k: velocity_hbm.at[pl.ds(1, 2), k], planes_vel, plane_send.at[0], plane_recv.at[0]
-    )
-    plane_begin, plane_arrive, plane_finish = exchange(
-        lambda k: stage.at[:, :, pl.ds(pl.multiple_of(8 * k, 8), 8)],
-        planes,
-        plane_send.at[1],
-        plane_recv.at[1],
-    )
-    vel_begin()
 
     def lead(n):
         return lax.broadcasted_iota(jnp.int32, (n, 8, 128), 0)
@@ -383,7 +402,7 @@
         after = sweep_leading(rad_ext[g], *rad_coef, rad_rate)
         for r in range(nr):
             put(stage, g, pl.ds(8 * r, 8), after[r])
-    plane_begin()
+        plane_exchanges[g][0]()
 
     vel_arrive()
     for slot in range(nr + 2):
@@ -433,22 +452,11 @@
     ):
         azimuth_coef[i] = coefficient
     azimuth_coef[3] = rate
-    hear(2)
-    pl.semaphore_signal(
-        token_sem.at[3], inc=1, device_id=(twin, rad, ang), device_id_type=MESH
-    )
-
-    plane_arrive()
-    for slot in range(nr + 2):
-        for g in range(groups):
-            for c in range(tiles):
-                for f in range(2):
-                    block[2 * g + f, slot * nt : (slot + 1) * nt, 128 * c : 128 * c + 128] = planes[
-                        slot, g, c, f * nt : (f + 1) * nt, :
-                    ]
-    fill_ghosts(block, range(fields))
+    pl.semaphore_wait(token_sem.at[2], 2)
+
     cells = fields * row_cells
-    for f in range(fields):
+
+    def sweep_field(f):
         q = block[f]
         change = sweep_rolled(q, polar_coef[0], polar_coef[1], polar_coef[2], 0)
         q = (q - polar_coef[3] * change)[nt : nt + row_cells]
@@ -466,6 +474,18 @@
             split[row : row + row_cells, 0:nphi] = coarse
             split[row : row + row_cells, nphi : 2 * nphi] = (part - coarse.astype(F32)).astype(BF16)
 
+    for g in range(groups):
+        plane_exchanges[g][1]()
+        for slot in range(nr + 2):
+            for c in range(tiles):
+                for f in range(2):
+                    block[2 * g + f, slot * nt : (slot + 1) * nt, 128 * c : 128 * c + 128] = planes[
+                        slot, g, c, f * nt : (f + 1) * nt, :
+                    ]
+        fill_ghosts(block, (2 * g, 2 * g + 1))
+        for f in range(2):
+            sweep_field(2 * g + f)
+
     def back_copy(step):
         other = lax.rem(member + step, nr)
         return pltpu.make_async_remote_copy(
@@ -479,52 +499,52 @@
 
     theta_tiles = 2 * G * tiles
 
-    def zone_copies():
-        copies = []
-        for side, target in ((0, 0), (1, n_ang - 1)):
-            copies.append(
-                pltpu.make_async_remote_copy(
-                    src_ref=zone_out.at[pl.ds(side * theta_tiles // 2, theta_tiles // 2)],
-                    dst_ref=theta_in.at[ang],
-                    send_sem=zone_send.at[n_ang + side],
-                    recv_sem=theta_recv,
-                    device_id=(twin, rad, target),
-                    device_id_type=MESH,
-                )
+    def theta_copy(side):
+        return pltpu.make_async_remote_copy(
+            src_ref=zone_out.at[pl.ds(side * theta_tiles // 2, theta_tiles // 2)],
+            dst_ref=theta_in.at[ang],
+            send_sem=zone_send.at[n_ang + side],
+            recv_sem=theta_recv,
+            device_id=(twin, rad, side * (n_ang - 1)),
+            device_id_type=MESH,
+        )
+
+    def phi_copy(target):
+        return pltpu.make_async_remote_copy(
+            src_ref=zone_out.at[theta_tiles + target // (n_ang // 2)],
+            dst_ref=phi_in.at[ang],
+            send_sem=zone_send.at[target],
+            recv_sem=phi_recv,
+            device_id=(twin, rad, target),
+            device_id_type=MESH,
+        )
+
+    def pick(first, last):
+        x = split[...]
+        for z in range(first, last, 256):
+            y = jnp.dot(x, onehot[:, z : z + 256], preferred_element_type=F32)
+            near = near_weight[:, z : z + 256].reshape(1, row_cells, 256)
+            far = far_weight[:, z : z + 256].reshape(1, row_cells, 256)
+            picked = near * y[:cells].reshape(fields, row_cells, 256) + far * y[cells:].reshape(
+                fields, row_cells, 256
             )
-        for target in range(n_ang):
-            copies.append(
-                pltpu.make_async_remote_copy(
-                    src_ref=zone_out.at[theta_tiles + target // (n_ang // 2)],
-                    dst_ref=phi_in.at[ang],
-                    send_sem=zone_send.at[target],
-                    recv_sem=phi_recv,
-                    device_id=(twin, rad, target),
-                    device_id_type=MESH,
-                )
-            )
-        return copies
-
-    x = split[...]
-    for z in range(0, zones, 256):
-        y = jnp.dot(x, onehot[:, z : z + 256], preferred_element_type=F32)
-        near = near_weight[:, z : z + 256].reshape(1, row_cells, 256)
-        far = far_weight[:, z : z + 256].reshape(1, row_cells, 256)
-        picked = near * y[:cells].reshape(fields, row_cells, 256) + far * y[cells:].reshape(
-            fields, row_cells, 256
-        )
-        picked = picked.reshape(fields, row_cells // 8, 8, 256).sum(axis=1).reshape(8 * fields, 256)
-        for half in range(2):
-            zone_sum[z // 128 + half] = picked[:, 128 * half : 128 * half + 128]
-    for z in range(zones // 128):
-        parts = [zone_sum[z, pl.ds(t, fields, stride=8), :] for t in range(8)]
-        while len(parts) > 1:
-            parts = [a + b for a, b in zip(parts[::2], parts[1::2])]
-        zone_out[z, 0:fields, :] = parts[0]
-    pl.semaphore_wait(token_sem.at[3], 1)
-    for copy in zone_copies():
-        copy.start()
-
+            picked = picked.reshape(fields, row_cells // 8, 8, 256).sum(axis=1)
+            picked = picked.reshape(8 * fields, 256)
+            for half in range(2):
+                zone_sum[z // 128 + half] = picked[:, 128 * half : 128 * half + 128]
+        for z in range(first // 128, last // 128):
+            parts = [zone_sum[z, pl.ds(t, fields, stride=8), :] for t in range(8)]
+            while len(parts) > 1:
+                parts = [a + b for a, b in zip(parts[::2], parts[1::2])]
+            zone_out[z, 0:fields, :] = parts[0]
+
+    half_zones = theta_tiles // 2 * 128
+    for side in range(2):
+        pick(side * half_zones, (side + 1) * half_zones)
+        theta_copy(side).start()
+    pick(2 * half_zones, zones)
+    for target in range(n_ang):
+        phi_copy(target).start()
     for step in range(1, nr):
         back_copy(step).start()
     pltpu.make_async_copy(back_out.at[member], result.at[member], back_recv).start()
@@ -577,11 +597,14 @@
     for g in range(groups):
         both(has_rad, rad_copies(g), wait_send)
     vel_finish()
-    plane_finish()
+    for g in range(groups):
+        plane_exchanges[g][2]()
     for step in range(1, nr):
         back_copy(step).wait_send()
-    for copy in zone_copies():
-        copy.wait_send()
+    for side in range(2):
+        theta_copy(side).wait_send()
+    for target in range(n_ang):
+        phi_copy(target).wait_send()
 
 
 def solution(mesh):
@@ -630,14 +653,14 @@
                 pltpu.SemaphoreType.DMA((4,)),
                 pltpu.SemaphoreType.DMA((n_halo,)),
                 pltpu.SemaphoreType.DMA((n_halo,)),
-                pltpu.SemaphoreType.DMA((2, 3 * nr)),
-                pltpu.SemaphoreType.DMA((2, 3)),
+                pltpu.SemaphoreType.DMA((groups + 1, 3 * nr)),
+                pltpu.SemaphoreType.DMA((groups + 1, 3)),
                 pltpu.SemaphoreType.DMA((n_ang + 2,)),
                 pltpu.SemaphoreType.DMA,
                 pltpu.SemaphoreType.DMA,
                 pltpu.SemaphoreType.DMA((nr,)),
                 pltpu.SemaphoreType.DMA,
-                pltpu.SemaphoreType.REGULAR((4,)),
+                pltpu.SemaphoreType.REGULAR((3,)),
             ],
             compiler_params=pltpu.CompilerParams(
                 collective_id=0, has_side_effects=True, vmem_limit_bytes=40 * 1024 * 1024

time: 42.9 us -> 40.2 us (0.937)
  Pallas kernels: 42.1 us -> 39.4 us
    pallas_call x1, Pallas kernels: 42.1 us -> 39.4 us  [body(): pl.pallas_call(functools.partial(kernel, sizes), out_shape=jax.ShapeDtype...]
where the time goes in v4:
time: 40.2 us; the launch traced here: 40.1 us
  Pallas kernels  39.4 us (98%)
  local copies, waits for them, and re-layouts  0.66 us (2%)
    pallas_call x1, Pallas kernels, body(): pl.pallas_call(functools.partial(kernel, sizes), out_shape=jax.ShapeDtype...  39.4 us

profile of v4, /device:TPU:9, one launch (start us, length us, event | category | flops | bytes accessed | tf_op | source)
XLA Modules:
  0.0 40.1 jit_solution(5985816716129148435)
XLA Ops:
  0.0 39.4 %shard_map.46 = f32[6,4,4,384]{3,2,1,0:T(4,128)S(1)} custom-call(f32[6,4,4,384]{3,2,1,0:T(4,128)} %bitcast.4, f32[3,4,4,384]{3,2,1,0:T(4,128)} %bitcast.5, s32[2,1792]{1,0:T(2,128)} %donor_hbm.1, f32[2,4,1792]{2,1,0:T(4,128)} %weight_hbm.1), custom_call_target="tpu_custom_call" | custom-call | tf_op jit(solution)/shard_map/pallas_call | solution.py:622
  39.4 0.7 %copy.6 = f32[1,6,4,4,384]{4,3,2,1,0:T(4,128)} copy(f32[1,6,4,4,384]{4,3,2,1,0:T(4,128)S(1)} %bitcast.3) | data formatting | bytes 294912
